TPU v7x, 32 devices: a whole 2x2x4 slice. The times are simulated.
32 devices in a mesh: dp: 4 (over y, core), fsdp: 8 (over z, x).
Axes of the slice: x: 2, y: 2, z: 4, core: 2. Of those that a mesh axis runs over, the one named last changes fastest.
Arguments:
- context: bfloat16 [16384, 1024], P(('dp', 'fsdp')), may hold values from -6 to 6
- residual: bfloat16 [16384, 2048], P(('dp', 'fsdp')), may hold values from -6 to 6
- out_weight: bfloat16 [1024, 2048], P('fsdp'), may hold values from -0.1875 to 0.1875
- norm_gain: float32 [2048], replicated, may hold values from 0.5 to 1.5
- user_vectors: bfloat16 [256, 2048], P(('dp', 'fsdp')), may hold values from -12 to 12
- positive: int32 [256], P(('dp', 'fsdp')), may hold values from 0 to 63
- item_ids: int32 [64], P(('dp', 'fsdp')), may hold values from 0 to 31
- item_counts: int32 [64], P(('dp', 'fsdp')), may hold values from 1 to 5000
- lengths: int32 [64], P(('dp', 'fsdp')), may hold values from 64 to 256
Outputs:
- mean_loss: float32 [], replicated
- residual_grad: bfloat16 [16384, 2048], P(('dp', 'fsdp'))
- context_grad: bfloat16 [16384, 1024], P(('dp', 'fsdp'))
- weight_grad: bfloat16 [1024, 2048], P('fsdp')
- norm_gain_grad: float32 [2048], replicated
- user_grad: bfloat16 [256, 2048], P(('dp', 'fsdp'))
All inputs are finite; a program needn't handle non-finite values.
Results may differ from a plain program's by a relative error of at most 0.015.
Values may be sent and summed in bfloat16 or wider, within the bound.
A program may use at most 128 MiB of HBM per device.

v0:
```python
import jax
import jax.numpy as jnp
from jax import lax
from jax.sharding import PartitionSpec as P

EPSILON = 1e-06
MASKED_FILL = -1e30


def contract_rows(left, right):
    return lax.dot_general(
        left, right, (((0,), (0,)), ((), ())), preferred_element_type=jnp.float32
    )


def contract_last(left, right):
    return lax.dot_general(
        left, right, (((1,), (1,)), ((), ())), preferred_element_type=jnp.float32
    )


def on_device(
    context, residual, out_weight, norm_gain, user_vectors, positive, item_ids, item_counts, lengths
):
    tok_rows, head_width = context.shape
    model_width = residual.shape[1]
    items_here = lengths.shape[0]
    item_length = tok_rows // items_here
    users_here = user_vectors.shape[0]
    devices_all = lax.axis_size("dp") * lax.axis_size("fsdp")
    columns = context
    attended = jnp.dot(
        columns,
        lax.all_gather(out_weight, "fsdp", axis=0, tiled=True),
        preferred_element_type=jnp.float32,
    )
    stream = residual.astype(jnp.float32) + attended
    inverse_root_mean = lax.rsqrt(jnp.mean(stream * stream, axis=-1, keepdims=True) + EPSILON)
    normed = stream * inverse_root_mean * norm_gain
    positions = jnp.arange(item_length, dtype=jnp.int32)
    inside = (positions[None, :] < lengths[:, None])[:, :, None]
    length_float = lengths.astype(jnp.float32)[:, None]
    normed_items = normed.reshape(items_here, item_length, model_width)
    pooled = jnp.sum(jnp.where(inside, normed_items, 0.0), axis=1) / length_float
    emb_scale = lax.rsqrt(jnp.mean(pooled * pooled, axis=-1, keepdims=True) + EPSILON)
    embedding = (pooled * emb_scale).astype(jnp.bfloat16)
    keys = jnp.stack([item_ids, item_counts], axis=1)
    keys_all = lax.all_gather(keys, ("dp", "fsdp"), axis=0, tiled=True)
    emb_all = lax.all_gather(embedding, ("dp", "fsdp"), axis=0, tiled=True)
    items_all = jnp.arange(keys_all.shape[0], dtype=jnp.int32)
    onehot = items_all[None, :] == positive[:, None]
    positive_id = jnp.sum(jnp.where(onehot, keys_all[None, :, 0], 0), axis=1)
    excluded = (keys_all[None, :, 0] == positive_id[:, None]) & jnp.logical_not(onehot)
    scores = contract_last(user_vectors, emb_all)
    log_counts = jnp.log(keys_all[:, 1].astype(jnp.float32))
    logits = jnp.where(excluded, MASKED_FILL, scores - log_counts[None, :])
    row_max = jnp.max(logits, axis=1, keepdims=True)
    weights = jnp.where(excluded, 0.0, jnp.exp(logits - row_max))
    row_total = jnp.sum(weights, axis=1, keepdims=True)
    log_total = row_max[:, 0] + jnp.log(row_total[:, 0])
    loss_part = jnp.sum(log_total - jnp.sum(jnp.where(onehot, logits, 0.0), axis=1))
    logit_grad = (weights / row_total - onehot.astype(jnp.float32)).astype(jnp.bfloat16)
    user_grad = jnp.dot(logit_grad, emb_all, preferred_element_type=jnp.float32).astype(
        jnp.bfloat16
    )
    emb_grad = lax.psum_scatter(
        contract_rows(logit_grad, user_vectors), ("dp", "fsdp"), scatter_dimension=0, tiled=True
    )
    pooled_grad = emb_scale * emb_grad - pooled * emb_scale**3 * jnp.mean(
        pooled * emb_grad, axis=-1, keepdims=True
    )
    normed_grad = jnp.where(inside, pooled_grad[:, None, :] / length_float[:, :, None], 0.0)
    normed_grad = normed_grad.reshape(tok_rows, model_width)
    gain_part = jnp.sum(normed_grad * stream * inverse_root_mean, axis=0)
    scaled = norm_gain * normed_grad
    stream_grad = inverse_root_mean * scaled - stream * inverse_root_mean**3 * jnp.mean(
        scaled * stream, axis=-1, keepdims=True
    )
    residual_grad = stream_grad.astype(jnp.bfloat16)
    context_grad = contract_last(
        residual_grad, lax.all_gather(out_weight, "fsdp", axis=0, tiled=True)
    )
    context_grad = context_grad.astype(jnp.bfloat16)
    columns = context
    group_part = lax.psum_scatter(
        contract_rows(columns, residual_grad).astype(jnp.bfloat16),
        "fsdp",
        scatter_dimension=0,
        tiled=True,
    )
    weight_grad = lax.psum(group_part, "dp")
    loss_sum, gain_grad = lax.psum((loss_part, gain_part), ("dp", "fsdp"))
    mean_loss = loss_sum / (users_here * devices_all)
    return (mean_loss, residual_grad, context_grad, weight_grad, gain_grad, user_grad)


def solution(mesh):
    placed = (
        P(("dp", "fsdp"), None),
        P(("dp", "fsdp"), None),
        P("fsdp", None),
        P(),
        P(("dp", "fsdp"), None),
        P(("dp", "fsdp")),
        P(("dp", "fsdp")),
        P(("dp", "fsdp")),
        P(("dp", "fsdp")),
    )
    return jax.shard_map(
        on_device,
        mesh=mesh,
        in_specs=placed,
        out_specs=(
            P(),
            P(("dp", "fsdp"), None),
            P(("dp", "fsdp"), None),
            P("fsdp", None),
            P(),
            P(("dp", "fsdp"), None),
        ),
        check_vma=False,
    )
```

profile of v0, /device:TPU:0, one launch (start us, length us, event | category | flops | bytes accessed | tf_op | source)
XLA Modules:
  0.0 452.8 jit_solution(3463987567773126831)
XLA Ops:
  7.2 0.7 all-gather.4.cloned.1.call-update
  8.0 0.7 convert_element_type.39
  8.6 0.7 pad_add_fusion
  9.3 0.1 copy.21
  9.4 72.2 %all-gather = s32[32,2,2]{2,1,0:T(2,128)S(1)} all-gather(s32[1,2,2]{2,1,0:T(2,128)S(1)} %bitcast.55), channel_id=1, replica_groups=mesh['dp'=4,'fsdp'=8] {'dp','fsdp'}, dimensions={0}, use_global_device_ids=true | all-gather | bytes 528 | tf_op jit(solution)/shard_map/all_gather | solution.py:48
  81.7 0.1 convert_log_fusion
  81.9 0.8 select_reduce_fusion.2
  82.7 0.7 iota_compare_fusion.1
  83.4 2.7 all-gather.4.cloned.1.call-done
  86.2 5.3 %multiply_reduce_fusion = (f32[512]{0:T(512)S(1)}, f32[512,2048]{1,0:T(8,128)S(1)}) fusion(bf16[512,1024]{1,0:T(8,128)(2,1)S(1)} %copy-done, bf16[1024,2048]{1,0:T(8,128)(2,1)} %all-gather.4.cloned.1.call-done, bf16[512,2048]{1,0:T(8,128)(2,1)} %param.10), kind=kOutput, calls=%fused_computation.13 | convolution fusion | flops 2151677440 | bytes 11536384 | tf_op jit(solution)/shard_map/dot_general | solution.py:32
  91.6 1.9 copy-done.1
  93.5 0.7 select_reduce_fusion
  94.2 0.2 multiply_reduce_fusion.2
  94.5 66.8 %all-gather.1 = bf16[32,2,2048]{2,1,0:T(2,128)(2,1)S(1)} all-gather(bf16[1,2,2048]{2,1,0:T(2,128)(2,1)S(1)} %fusion.11), channel_id=1, replica_groups=mesh['dp'=4,'fsdp'=8] {'dp','fsdp'}, dimensions={0}, use_global_device_ids=true | all-gather | bytes 270336 | tf_op jit(solution)/shard_map/all_gather | solution.py:49
  161.2 0.1 reshape.103
  161.3 0.3 fusion.16
  161.6 0.2 fusion.14
  161.8 1.1 fusion.15
  163.1 126.0 %all-reduce.7.cloned.1.call-done = f32[64,2048]{1,0:T(8,128)} async-done(((f32[64,2048]{1,0:T(8,128)}), f32[64,2048]{1,0:T(8,128)}) %all-reduce.7.cloned.1.call-update) | async-done | bytes 524304
  289.1 1.1 multiply_reduce_fusion.1
  290.2 1.1 subtract_divide_fusion
  291.3 3.3 fusion.8
  294.7 1.3 fusion.5
  296.0 4.4 convert_bitcast_fusion
  300.3 6.5 %copy.25 = bf16[1024,2048]{1,0:T(8,128)(2,1)} copy(bf16[1024,2048]{0,1:T(8,128)(2,1)} %convert_bitcast_fusion) | data formatting | bytes 8388608
  306.9 0.6 subtract_reduce_fusion
  307.5 0.8 convolution_convert_fusion
  308.4 86.0 %reduce-scatter.4.cloned.1.call-done = bf16[128,2048]{1,0:T(8,128)(2,1)} async-done(((bf16[1024,2048]{1,0:T(8,128)(2,1)}), bf16[128,2048]{1,0:T(8,128)(2,1)}) %reduce-scatter.4.cloned.1.call-update) | async-done | bytes 524304
  394.4 2.0 copy.26
  396.4 5.5 %convolution_convert_fusion.1 = bf16[512,1024]{1,0:T(8,128)(2,1)} fusion(bf16[512,2048]{1,0:T(8,128)(2,1)S(1)} %fusion.5, bf16[1024,2048]{1,0:T(8,128)(2,1)} %all-gather.4.cloned.1.call-done), kind=kOutput, calls=%fused_computation.16 | convolution fusion | flops 2148007936 | bytes 7340032 | tf_op jit(solution)/shard_map/dot_general | solution.py:17
  402.0 40.4 %all-reduce.1 = (f32[]{:T(128)}, f32[2048]{0:T(1024)}) all-reduce(f32[]{:T(128)} %subtract_reduce_fusion, f32[2048]{0:T(1024)S(1)} %get-tuple-element.24), channel_id=1, replica_groups=mesh['dp'=4,'fsdp'=8] {'dp','fsdp'}, use_global_device_ids=true, to_apply=%region_8.9 | all-reduce | flops 2049 | bytes 16392 | tf_op jit(solution)/shard_map/psum | solution.py:92
  443.1 2.0 copy.23
  (29 shorter events, 0.5 us)
Async XLA Ops:
  7.2 79.0 %copy-start = (bf16[512,1024]{1,0:T(8,128)(2,1)S(1)}, bf16[512,1024]{1,0:T(8,128)(2,1)}, u32[]{:S(2)}) copy-start(bf16[512,1024]{1,0:T(8,128)(2,1)} %param.9) | copy-start | bytes 3145732
  7.2 79.0 %all-gather.4.cloned.1.call-start = ((), (), s32[]{:S(2)}) async-start(), calls=%async_computation.1 | async-start | bytes 4718592 | tf_op jit(solution)/shard_map/all_gather | solution.py:34
  7.9 281.2 %all-reduce.7.cloned.1.call-start = ((), (), s32[]{:S(2)}) async-start(), calls=%async_computation.4 | async-start | bytes 1048576
  83.4 10.1 %copy-start.4 = (f32[2048]{0:T(1024)S(1)}, f32[2048]{0:T(1024)}, u32[]{:S(2)}) copy-start(f32[2048]{0:T(1024)} %param.12) | copy-start | bytes 24580
  91.5 2.0 copy-start.1
  91.5 69.8 %copy-start.5 = (bf16[8,2048]{1,0:T(8,128)(2,1)S(1)}, bf16[8,2048]{1,0:T(8,128)(2,1)}, u32[]{:S(2)}) copy-start(bf16[8,2048]{1,0:T(8,128)(2,1)} %param.13) | copy-start | bytes 98308
  91.5 69.8 %copy-start.6 = (s32[8]{0:T(128)S(1)}, s32[8]{0:T(128)}, u32[]{:S(2)}) copy-start(s32[8]{0:T(128)} %param.14) | copy-start | bytes 100
  163.0 231.4 %reduce-scatter.4.cloned.1.call-start = ((), (), s32[]{:S(2)}) async-start(), calls=%async_computation.3 | async-start | bytes 4718592
  289.1 5.6 %copy-start.2 = (f32[512,2048]{1,0:T(8,128)S(1)}, f32[512,2048]{1,0:T(8,128)}, u32[]{:S(2)}) copy-start(f32[512,2048]{1,0:T(8,128)} %copy-done.1) | copy-start | bytes 12582916
  296.0 100.5 %copy-start.3 = (bf16[512,2048]{1,0:T(8,128)(2,1)}, bf16[512,2048]{1,0:T(8,128)(2,1)S(1)}, u32[]{:S(2)}) copy-start(bf16[512,2048]{1,0:T(8,128)(2,1)S(1)} %fusion.5) | copy-start | bytes 6291460
  306.9 136.2 %all-reduce.5.cloned.1.call-start = ((), (), s32[]{:S(2)}) async-start(), calls=%async_computation.2 | async-start | bytes 1048576 | tf_op jit(solution)/shard_map/psum | solution.py:91
Sparse Core Ops, SparseCore 0:
  10.1 75.9 all-gather.3
  163.1 125.9 all-reduce.6
  307.0 87.3 reduce-scatter.3
  397.1 33.0 all-reduce.4
where the time goes:
time: 453 us
  waiting for transfers between devices  215 us (47%)
  blocking collectives  179 us (40%)
  matrix products  17.5 us (4%)
  between operations  15.7 us (3%)
  local copies, waits for them, and re-layouts  12.9 us (3%)
  other arithmetic  11.6 us (3%)
    unnamed x6, waiting for transfers between devices  213 us
    all_gather x1, blocking collectives, on_device(): keys_all = lax.all_gather(keys, ('dp', 'fsdp'), axis=0, tiled=True)  72.2 us
    all_gather x1, blocking collectives, on_device(): emb_all = lax.all_gather(embedding, ('dp', 'fsdp'), axis=0, tiled=True)  66.8 us
    psum x1, blocking collectives, on_device(): loss_sum, gain_grad = lax.psum((loss_part, gain_part), ('dp', 'fsdp'))  40.4 us
    unnamed x20, local copies, waits for them, and re-layouts  12.8 us
  transfers between devices with their start and end apart: 4, of which 3 were waited for; matrix products, arithmetic and copies ran while one was open for 2% of the time, Pallas kernels for 0%

commit v1 on v0

v1 whole, which is shorter than its diff:
```python
import functools

import jax
import jax.numpy as jnp
from jax import lax
from jax.experimental import pallas as pl
from jax.experimental.pallas import tpu as pltpu
from jax.sharding import PartitionSpec as P

EPSILON = 1e-06
MASKED_FILL = -1e30
MESH = pl.DeviceIdType.MESH
CHUNKS = 4


def contract_rows(left, right):
    return lax.dot_general(
        left, right, (((0,), (0,)), ((), ())), preferred_element_type=jnp.float32
    )


def contract_last(left, right):
    return lax.dot_general(
        left, right, (((1,), (1,)), ((), ())), preferred_element_type=jnp.float32
    )


def ring_place(index, count):
    return jnp.where(index % 2 == 0, index // 2, count - 1 - index // 2)


def ring_index(place, count):
    return jnp.where(place < count // 2, 2 * place, 2 * (count - 1 - place) + 1)


def greet(devices):
    barrier = pltpu.get_barrier_semaphore()
    for device in devices:
        pl.semaphore_signal(barrier, inc=1, device_id=device, device_id_type=MESH)
    pl.semaphore_wait(barrier, len(devices))


def greet_all(groups, ring, me):
    total = groups * ring
    barrier = pltpu.get_barrier_semaphore()

    def signal(k, carry):
        peer = lax.rem(me + k, total)
        pl.semaphore_signal(
            barrier, inc=1, device_id=(peer // ring, lax.rem(peer, ring)), device_id_type=MESH
        )
        return carry

    lax.fori_loop(1, total, signal, 0)
    pl.semaphore_wait(barrier, total - 1)


def remote(src, dst, send_sem, recv_sem, device):
    return pltpu.make_async_remote_copy(
        src_ref=src,
        dst_ref=dst,
        send_sem=send_sem,
        recv_sem=recv_sem,
        device_id=device,
        device_id_type=MESH,
    )


def gather_kernel(
    groups, ring, w_in, u_in, k_in, w_out, u_out, k_out,
    own_sem, w_send, w_recv, p_send, p_recv, u_send, u_recv, k_send, k_recv,
    du_send, du_recv, dk_send, dk_recv,
):
    group, index = lax.axis_index("dp"), lax.axis_index("fsdp")
    core = lax.rem(group, 2)
    partner = group + 1 - 2 * core
    step = 1 - 2 * core
    place = ring_place(index, ring)
    rows = w_in.shape[0]
    half = rows // 2
    part = half // CHUNKS
    following = ring_index(lax.rem(place + ring + step, ring), ring)
    previous = ring_index(lax.rem(place + ring - step, ring), ring)

    def owner(s, way=step):
        return ring_index(lax.rem(place + ring * ring - s * way, ring), ring)

    def w_slice(who, c, side=core):
        start = pl.multiple_of(who * rows + side * half + c * part, part)
        return w_out.at[pl.ds(start, part), :]

    greet(
        [(lax.rem(group + k, groups), index) for k in range(1, groups)]
        + [(group, following), (group, previous)]
    )
    own = [
        pltpu.make_async_copy(
            w_in, w_out.at[pl.ds(pl.multiple_of(index * rows, rows), rows), :], own_sem.at[0]
        ),
        pltpu.make_async_copy(u_in, u_out.at[group * ring + index], own_sem.at[1]),
        pltpu.make_async_copy(k_in, k_out.at[group * ring + index], own_sem.at[2]),
    ]
    for copy in own:
        copy.start()
    for copy in own:
        copy.wait()

    def w_ring(s, c):
        ref = w_slice(owner(s), c)
        return remote(ref, ref, w_send.at[s, c], w_recv.at[s, c], (group, following))

    def w_ring_in(s, c):
        ref = w_slice(owner(s + 1), c)
        return remote(ref, ref, w_send.at[s, c], w_recv.at[s, c], (group, following))

    def w_part(s, c):
        ref = w_slice(owner(s + 1), c)
        return remote(ref, ref, p_send.at[s, c], p_recv.at[s, c], (partner, index))

    def w_part_in(s, c):
        ref = w_slice(owner(s + 1, -step), c, 1 - core)
        return remote(ref, ref, p_send.at[s, c], p_recv.at[s, c], (partner, index))

    small = ((u_out, u_send, u_recv, du_send, du_recv), (k_out, k_send, k_recv, dk_send, dk_recv))

    def s_ring(a, s, shift):
        out, send, recv, _, _ = small[a]
        ref = out.at[group * ring + owner(s + shift)]
        return remote(ref, ref, send.at[s], recv.at[s], (group, following))

    def s_out(a, s, k):
        out, _, _, send, recv = small[a]
        ref = out.at[group * ring + owner(s)]
        peer = lax.rem(group + k, groups)
        return remote(ref, ref, send.at[s, k - 1], recv.at[s, k - 1], (peer, index))

    def s_in(a, s, k):
        out, _, _, send, recv = small[a]
        source = lax.rem(group + groups - k, groups)
        way = 1 - 2 * lax.rem(source, 2)
        ref = out.at[source * ring + owner(s, way)]
        return remote(ref, ref, send.at[s, k - 1], recv.at[s, k - 1], (source, index))

    for c in range(CHUNKS):
        w_ring(0, c).start()
    for a in (0, 1):
        s_ring(a, 0, 0).start()
        for k in range(1, groups):
            s_out(a, 0, k).start()

    def forward(s, carry):
        for c in range(CHUNKS):
            w_ring_in(s - 1, c).wait_recv()
            w_ring(s, c).start()
            w_part(s - 1, c).start()
        for a in (0, 1):
            s_ring(a, s - 1, 1).wait_recv()
            s_ring(a, s, 0).start()
            for k in range(1, groups):
                s_out(a, s, k).start()
        return carry

    lax.fori_loop(1, ring - 1, forward, 0)
    last = ring - 1
    for c in range(CHUNKS):
        w_ring_in(last - 1, c).wait_recv()
        w_part(last - 1, c).start()
    for a in (0, 1):
        s_ring(a, last - 1, 1).wait_recv()
        for k in range(1, groups):
            s_out(a, last, k).start()

    def finish(s, carry):
        for c in range(CHUNKS):
            w_ring(s, c).wait_send()
            w_part(s, c).wait_send()
            w_part_in(s, c).wait_recv()
        for a in (0, 1):
            s_ring(a, s, 0).wait_send()
        return carry

    lax.fori_loop(0, ring - 1, finish, 0)

    def finish_small(s, carry):
        for a in (0, 1):
            for k in range(1, groups):
                s_out(a, s, k).wait_send()
                s_in(a, s, k).wait_recv()
        return carry

    lax.fori_loop(0, ring, finish_small, 0)


def gather_inputs(groups, ring, weight, users, keys):
    total = groups * ring
    rows, width = weight.shape
    dma = pltpu.SemaphoreType.DMA
    vmem = pl.BlockSpec(memory_space=pltpu.VMEM)
    anywhere = pl.BlockSpec(memory_space=pl.ANY)
    return pl.pallas_call(
        functools.partial(gather_kernel, groups, ring),
        out_shape=(
            jax.ShapeDtypeStruct((ring * rows, width), weight.dtype),
            jax.ShapeDtypeStruct((total,) + users.shape, users.dtype),
            jax.ShapeDtypeStruct((total,) + keys.shape, keys.dtype),
        ),
        in_specs=[anywhere, anywhere, anywhere],
        out_specs=(vmem, vmem, vmem),
        scratch_shapes=[dma((3,))]
        + [dma((ring - 1, CHUNKS))] * 4
        + [dma((ring - 1,))] * 4
        + [dma((ring, groups - 1))] * 4,
        compiler_params=pltpu.CompilerParams(
            collective_id=0, has_side_effects=True, vmem_limit_bytes=32 << 20
        ),
        name="gather_inputs",
    )(weight, users, keys)


def share_kernel(groups, ring, x_in, x_out, own_sem, send_sem, recv_sem):
    total = groups * ring
    me = lax.axis_index("dp") * ring + lax.axis_index("fsdp")
    greet_all(groups, ring, me)

    def push(k):
        peer = lax.rem(me + k, total)
        return remote(
            x_in, x_out.at[me], send_sem.at[k - 1], recv_sem.at[k - 1],
            (peer // ring, lax.rem(peer, ring)),
        )

    def pull(k):
        source = lax.rem(me + total - k, total)
        return remote(
            x_in, x_out.at[source], send_sem.at[k - 1], recv_sem.at[k - 1],
            (source // ring, lax.rem(source, ring)),
        )

    def start(k, carry):
        push(k).start()
        return carry

    def finish(k, carry):
        push(k).wait_send()
        pull(k).wait_recv()
        return carry

    lax.fori_loop(1, total, start, 0)
    own = pltpu.make_async_copy(x_in, x_out.at[me], own_sem)
    own.start()
    own.wait()
    lax.fori_loop(1, total, finish, 0)


def share(groups, ring, block):
    total = groups * ring
    dma = pltpu.SemaphoreType.DMA
    vmem = pl.BlockSpec(memory_space=pltpu.VMEM)
    return pl.pallas_call(
        functools.partial(share_kernel, groups, ring),
        out_shape=jax.ShapeDtypeStruct((total,) + block.shape, block.dtype),
        in_specs=[vmem],
        out_specs=vmem,
        scratch_shapes=[dma, dma((total - 1,)), dma((total - 1,))],
        compiler_params=pltpu.CompilerParams(collective_id=1, has_side_effects=True),
        name="share",
    )(block)


def reduce_kernel(
    groups, ring, part_in, gain_in, out, gain_out,
    cross, held, arrived, totals,
    own_sem, g_send, g_recv, x_send, x_recv, r_send, r_recv, t_send, t_recv, o_send, o_recv,
):
    total = groups * ring
    group, index = lax.axis_index("dp"), lax.axis_index("fsdp")
    me = group * ring + index
    core = lax.rem(group, 2)
    partner = group + 1 - 2 * core
    step = 1 - 2 * core
    place = ring_place(index, ring)
    rows = part_in.shape[0] // ring
    half = rows // 2
    piece = half // CHUNKS
    lines = groups // 2
    line = group // 2
    following = ring_index(lax.rem(place + ring + step, ring), ring)

    def owner(s, way=step):
        return ring_index(lax.rem(place + ring * ring - (s + 1) * way, ring), ring)

    greet_all(groups, ring, me)

    def cross_out(s):
        who = owner(s, -step)
        start = pl.multiple_of(who * rows + (1 - core) * half, half)
        return remote(
            part_in.at[pl.ds(start, half), :], cross.at[s], x_send.at[s], x_recv.at[s],
            (partner, index),
        )

    def start_cross(s, carry):
        cross_out(s).start()
        return carry

    lax.fori_loop(0, ring, start_cross, 0)

    def gain_push(k):
        peer = lax.rem(me + k, total)
        return remote(
            gain_in, gain_out.at[me], g_send.at[k - 1], g_recv.at[k - 1],
            (peer // ring, lax.rem(peer, ring)),
        )

    def gain_pull(k):
        source = lax.rem(me + total - k, total)
        return remote(
            gain_in, gain_out.at[source], g_send.at[k - 1], g_recv.at[k - 1],
            (source // ring, lax.rem(source, ring)),
        )

    def start_gain(k, carry):
        gain_push(k).start()
        return carry

    lax.fori_loop(1, total, start_gain, 0)
    own = pltpu.make_async_copy(gain_in, gain_out.at[me], own_sem)
    own.start()

    def ring_copy(s, c):
        at = pl.ds(c * piece, piece)
        return remote(
            held.at[s, at, :], arrived.at[s, at, :], r_send.at[s, c], r_recv.at[s, c],
            (group, following),
        )

    def local_term(s, c):
        start = pl.multiple_of(owner(s) * rows + core * half + c * piece, piece)
        mine = part_in[pl.ds(start, piece), :].astype(jnp.float32)
        return mine + cross[s, pl.ds(c * piece, piece), :].astype(jnp.float32)

    cross_out(0).wait_recv()
    for c in range(CHUNKS):
        held[0, pl.ds(c * piece, piece), :] = local_term(0, c).astype(held.dtype)
        ring_copy(0, c).start()

    def pass_on(s, carry):
        cross_out(s).wait_recv()
        for c in range(CHUNKS):
            at = pl.ds(c * piece, piece)
            term = local_term(s, c)
            ring_copy(s - 1, c).wait_recv()
            held[s, at, :] = (term + arrived[s - 1, at, :].astype(jnp.float32)).astype(held.dtype)
            ring_copy(s, c).start()
        return carry

    lax.fori_loop(1, ring - 1, pass_on, 0)
    last = ring - 1
    cross_out(last).wait_recv()

    def total_copy(k, c):
        at = pl.ds(c * piece, piece)
        ref = totals.at[line, at, :]
        return remote(
            ref, ref, t_send.at[k - 1, c], t_recv.at[k - 1, c],
            (lax.rem(group + 2 * k, groups), index),
        )

    def total_in(k, c):
        at = pl.ds(c * piece, piece)
        source = lax.rem(group + groups - 2 * k, groups)
        ref = totals.at[source // 2, at, :]
        return remote(ref, ref, t_send.at[k - 1, c], t_recv.at[k - 1, c], (source, index))

    for c in range(CHUNKS):
        at = pl.ds(c * piece, piece)
        term = local_term(last, c)
        ring_copy(last - 1, c).wait_recv()
        totals[line, at, :] = (term + arrived[last - 1, at, :].astype(jnp.float32)).astype(
            totals.dtype
        )
        for k in range(1, lines):
            total_copy(k, c).start()

    def out_copy(c, side):
        ref = out.at[pl.ds(pl.multiple_of(side * half + c * piece, piece), piece), :]
        return remote(ref, ref, o_send.at[c], o_recv.at[c], (partner, index))

    for c in range(CHUNKS):
        at = pl.ds(c * piece, piece)
        for k in range(1, lines):
            total_in(k, c).wait_recv()
        value = totals[0, at, :].astype(jnp.float32)
        for j in range(1, lines):
            value = value + totals[j, at, :].astype(jnp.float32)
        out[pl.ds(pl.multiple_of(core * half + c * piece, piece), piece), :] = value.astype(
            out.dtype
        )
        out_copy(c, core).start()

    def finish_cross(s, carry):
        cross_out(s).wait_send()
        return carry

    lax.fori_loop(0, ring, finish_cross, 0)

    def finish_ring(s, carry):
        for c in range(CHUNKS):
            ring_copy(s, c).wait_send()
        return carry

    lax.fori_loop(0, ring - 1, finish_ring, 0)
    own.wait()

    def finish_gain(k, carry):
        gain_push(k).wait_send()
        gain_pull(k).wait_recv()
        return carry

    lax.fori_loop(1, total, finish_gain, 0)
    for c in range(CHUNKS):
        for k in range(1, lines):
            total_copy(k, c).wait_send()
        out_copy(c, core).wait_send()
        out_copy(c, 1 - core).wait_recv()


def reduce_weight(groups, ring, partial, gain):
    total = groups * ring
    rows = partial.shape[0] // ring
    half, width = rows // 2, partial.shape[1]
    dma = pltpu.SemaphoreType.DMA
    vmem = pl.BlockSpec(memory_space=pltpu.VMEM)
    return pl.pallas_call(
        functools.partial(reduce_kernel, groups, ring),
        out_shape=(
            jax.ShapeDtypeStruct((rows, width), partial.dtype),
            jax.ShapeDtypeStruct((total,) + gain.shape, gain.dtype),
        ),
        in_specs=[vmem, vmem],
        out_specs=(vmem, vmem),
        scratch_shapes=[
            pltpu.VMEM((ring, half, width), partial.dtype),
            pltpu.VMEM((ring - 1, half, width), partial.dtype),
            pltpu.VMEM((ring - 1, half, width), partial.dtype),
            pltpu.VMEM((groups // 2, half, width), partial.dtype),
            dma,
            dma((total - 1,)),
            dma((total - 1,)),
            dma((ring,)),
            dma((ring,)),
            dma((ring - 1, CHUNKS)),
            dma((ring - 1, CHUNKS)),
            dma((groups // 2 - 1, CHUNKS)),
            dma((groups // 2 - 1, CHUNKS)),
            dma((CHUNKS,)),
            dma((CHUNKS,)),
        ],
        compiler_params=pltpu.CompilerParams(
            collective_id=2, has_side_effects=True, vmem_limit_bytes=40 << 20
        ),
        name="reduce_weight",
    )(partial, gain)


def on_device(
    groups, ring,
    context, residual, out_weight, norm_gain, user_vectors, positive, item_ids, item_counts, lengths
):
    tok_rows, head_width = context.shape
    model_width = residual.shape[1]
    items_here = lengths.shape[0]
    item_length = tok_rows // items_here
    users_here = user_vectors.shape[0]
    devices_all = groups * ring
    lanes = 128 * pl.cdiv(max(users_here, items_here), 128)
    keys = jnp.stack(
        [jnp.pad(row, (0, lanes - row.shape[0])) for row in (positive, item_ids, item_counts)]
    )
    keys = jnp.pad(keys, ((0, 5), (0, 0)))
    weight_all, users_all, keys_all = gather_inputs(groups, ring, out_weight, user_vectors, keys)
    users_all = users_all.reshape(devices_all * users_here, model_width)
    positive_all = keys_all[:, 0, :users_here].reshape(-1)
    ids_all = keys_all[:, 1, :items_here].reshape(-1)
    counts_all = keys_all[:, 2, :items_here].reshape(-1)
    attended = jnp.dot(context, weight_all, preferred_element_type=jnp.float32)
    stream = residual.astype(jnp.float32) + attended
    inverse_root_mean = lax.rsqrt(jnp.mean(stream * stream, axis=-1, keepdims=True) + EPSILON)
    normed = stream * inverse_root_mean * norm_gain
    positions = jnp.arange(item_length, dtype=jnp.int32)
    inside = (positions[None, :] < lengths[:, None])[:, :, None]
    length_float = lengths.astype(jnp.float32)[:, None]
    normed_items = normed.reshape(items_here, item_length, model_width)
    pooled = jnp.sum(jnp.where(inside, normed_items, 0.0), axis=1) / length_float
    emb_scale = lax.rsqrt(jnp.mean(pooled * pooled, axis=-1, keepdims=True) + EPSILON)
    embedding = (pooled * emb_scale).astype(jnp.bfloat16)
    emb_all = share(groups, ring, embedding).reshape(devices_all * items_here, model_width)
    me = lax.axis_index("dp") * ring + lax.axis_index("fsdp")
    items_all = jnp.arange(ids_all.shape[0], dtype=jnp.int32)
    onehot = items_all[None, :] == positive_all[:, None]
    positive_id = jnp.sum(jnp.where(onehot, ids_all[None, :], 0), axis=1)
    excluded = (ids_all[None, :] == positive_id[:, None]) & jnp.logical_not(onehot)
    scores = contract_last(users_all, emb_all)
    log_counts = jnp.log(counts_all.astype(jnp.float32))
    logits = jnp.where(excluded, MASKED_FILL, scores - log_counts[None, :])
    row_max = jnp.max(logits, axis=1, keepdims=True)
    weights = jnp.where(excluded, 0.0, jnp.exp(logits - row_max))
    row_total = jnp.sum(weights, axis=1, keepdims=True)
    log_total = row_max[:, 0] + jnp.log(row_total[:, 0])
    mean_loss = jnp.mean(log_total - jnp.sum(jnp.where(onehot, logits, 0.0), axis=1))
    logit_grad = (weights / row_total - onehot.astype(jnp.float32)).astype(jnp.bfloat16)
    own_users = lax.dynamic_slice_in_dim(logit_grad, me * users_here, users_here, axis=0)
    user_grad = jnp.dot(own_users, emb_all, preferred_element_type=jnp.float32).astype(
        jnp.bfloat16
    )
    own_items = lax.dynamic_slice_in_dim(logit_grad, me * items_here, items_here, axis=1)
    emb_grad = contract_rows(own_items, users_all)
    pooled_grad = emb_scale * emb_grad - pooled * emb_scale**3 * jnp.mean(
        pooled * emb_grad, axis=-1, keepdims=True
    )
    normed_grad = jnp.where(inside, pooled_grad[:, None, :] / length_float[:, :, None], 0.0)
    normed_grad = normed_grad.reshape(tok_rows, model_width)
    gain_part = jnp.sum(normed_grad * stream * inverse_root_mean, axis=0)
    scaled = norm_gain * normed_grad
    stream_grad = inverse_root_mean * scaled - stream * inverse_root_mean**3 * jnp.mean(
        scaled * stream, axis=-1, keepdims=True
    )
    residual_grad = stream_grad.astype(jnp.bfloat16)
    context_grad = contract_last(residual_grad, weight_all).astype(jnp.bfloat16)
    partial = contract_rows(context, residual_grad).astype(jnp.bfloat16)
    weight_grad, gain_all = reduce_weight(groups, ring, partial, gain_part[None, :])
    gain_grad = jnp.sum(gain_all[:, 0, :], axis=0)
    return (mean_loss, residual_grad, context_grad, weight_grad, gain_grad, user_grad)


def solution(mesh):
    placed = (
        P(("dp", "fsdp"), None),
        P(("dp", "fsdp"), None),
        P("fsdp", None),
        P(),
        P(("dp", "fsdp"), None),
        P(("dp", "fsdp")),
        P(("dp", "fsdp")),
        P(("dp", "fsdp")),
        P(("dp", "fsdp")),
    )
    return jax.shard_map(
        functools.partial(on_device, mesh.shape["dp"], mesh.shape["fsdp"]),
        mesh=mesh,
        in_specs=placed,
        out_specs=(
            P(),
            P(("dp", "fsdp"), None),
            P(("dp", "fsdp"), None),
            P("fsdp", None),
            P(),
            P(("dp", "fsdp"), None),
        ),
        check_vma=False,
    )
```

time: 453 us -> 123 us (0.27)
  waiting for transfers between devices: 215 us -> 0 us
  blocking collectives: 179 us -> 0 us
  Pallas kernels: 0 us -> 87.3 us
  between operations: 15.7 us -> 2.61 us
  matrix products: 17.5 us -> 12.8 us
    unnamed x6 -> x0, waiting for transfers between devices: 213 us -> none
    all_gather x2 -> x0, blocking collectives: 139 us -> none  [the longest x1 72.2 us: on_device(): keys_all = lax.all_gather(keys, ('dp', 'fsdp'), axis=0, tiled=True)]
    pallas_call x0 -> x3, Pallas kernels: none -> 87.3 us  [the longest x1 38.7 us: reduce_weight(): pl.pallas_call(functools.partial(reduce_kernel, groups, ring), out_shape=...]
    psum x1 -> x0, blocking collectives: 40.4 us -> none  [on_device(): loss_sum, gain_grad = lax.psum((loss_part, gain_part), ('dp', 'fsdp'))]
    unnamed x20 -> x19, local copies, waits for them, and re-layouts: 12.8 us -> 7.36 us
  transfers between devices with their start and end apart: 4 -> 0, of which waited for: 3 -> 0; matrix products, arithmetic and copies ran while one was open for 2% -> 0% of each run, Pallas kernels for 0% -> 0%
where the time goes in v1:
time: 123 us
  Pallas kernels  87.3 us (71%)
  matrix products  12.8 us (10%)
  local copies, waits for them, and re-layouts  10.2 us (8%)
  other arithmetic  9.67 us (8%)
  between operations  2.61 us (2%)
    pallas_call x1, Pallas kernels, reduce_weight(): pl.pallas_call(functools.partial(reduce_kernel, groups, ring), out_shape=...  38.7 us
    pallas_call x1, Pallas kernels, gather_inputs(): pl.pallas_call(functools.partial(gather_kernel, groups, ring), out_shape=...  35.8 us
    pallas_call x1, Pallas kernels, share(): pl.pallas_call(functools.partial(share_kernel, groups, ring), out_shape=j...  12.8 us
    unnamed x19, local copies, waits for them, and re-layouts  7.36 us
    dot_general x1, matrix products, on_device(): attended = jnp.dot(context, weight_all, preferred_element_type=jnp.float32)  5.35 us
    dot_general x2, matrix products, contract_last(): lax.dot_general(left, right, (((1,), (1,)), ((), ())), preferred_element_...  3.82 us
    reduce_sum x1, other arithmetic, on_device(): gain_part = jnp.sum(normed_grad * stream * inverse_root_mean, axis=0)  3.5 us
    dot_general x2, matrix products, contract_rows(): lax.dot_general(left, right, (((0,), (0,)), ((), ())), preferred_element_...  2.79 us

profile of v1, /device:TPU:0, one launch (start us, length us, event | category | flops | bytes accessed | tf_op | source)
XLA Modules:
  0.0 122.5 jit_solution(8685719402467023664)
XLA Ops:
  0.7 0.7 convert_element_type.38
  1.4 0.7 pad_bitcast_fusion.2
  2.1 0.7 iota_compare_fusion.1
  2.8 0.7 pad_bitcast_fusion
  3.5 1.0 copy-done.1
  4.5 0.8 copy-done.2
  5.3 35.8 %gather_inputs.1 = (bf16[1024,2048]{1,0:T(8,128)(2,1)S(1)}, bf16[32,8,2048]{2,1,0:T(8,128)(2,1)S(1)}, s32[32,8,128]{2,1,0:T(8,128)S(1)}) custom-call(bf16[128,2048]{1,0:T(8,128)(2,1)S(1)} %copy-done.1, bf16[8,2048]{1,0:T(8,128)(2,1)S(1)} %copy-done.2, s32[8,128]{1,0:T(8,128)S(1)} %pad.18.k_in), custom_call_target="tpu_custom_call" | custom-call | tf_op jit(solution)/shard_map/gather_inputs/pallas_call | solution.py:200
  41.1 1.9 %copy-done.3 = bf16[1024,2048]{1,0:T(8,128)(2,1)} copy-done((bf16[1024,2048]{1,0:T(8,128)(2,1)}, bf16[1024,2048]{1,0:T(8,128)(2,1)S(1)}, u32[]{:S(2)}) %copy-start.3) | copy-done | bytes 4194328
  43.1 0.1 log.14
  43.3 0.1 eq.30
  43.5 0.1 select_reduce_fusion.2
  43.7 5.3 %multiply_reduce_fusion = (f32[512]{0:T(512)S(1)}, f32[512,2048]{1,0:T(8,128)S(1)}) fusion(bf16[512,1024]{1,0:T(8,128)(2,1)S(1)} %copy-done, bf16[1024,2048]{1,0:T(8,128)(2,1)} %copy-done.3, bf16[512,2048]{1,0:T(8,128)(2,1)} %param.10), kind=kOutput, calls=%fused_computation.14 | convolution fusion | flops 2151677440 | bytes 11536384 | tf_op jit(solution)/shard_map/dot_general | solution.py:486
  49.0 2.0 %copy-done.5 = f32[512,2048]{1,0:T(8,128)} copy-done((f32[512,2048]{1,0:T(8,128)}, f32[512,2048]{1,0:T(8,128)S(1)}, u32[]{:S(2)}) %copy-start.5) | copy-done | bytes 4194328
  51.0 0.7 select_reduce_fusion
  51.7 0.2 multiply_reduce_fusion.2
  51.9 0.7 multiply_convert_fusion.x_in
  52.6 12.8 %share.1 = bf16[32,2,2048]{2,1,0:T(2,128)(2,1)} custom-call(bf16[2,2048]{1,0:T(2,128)(2,1)} %multiply_convert_fusion.x_in), custom_call_target="tpu_custom_call" | custom-call | tf_op jit(solution)/shard_map/share/pallas_call | solution.py:259
  65.3 1.0 reshape.107
  66.4 0.5 fusion.20
  66.9 0.1 fusion.15
  67.0 0.1 subtract_convert_fusion
  67.1 0.4 multiply_reduce_fusion.1
  67.4 0.9 convolution_convert_fusion
  68.3 0.6 subtract_reduce_fusion
  69.7 3.5 %fusion.8 = (f32[2048]{0:T(1024)S(1)}, f32[512]{0:T(512)S(1)}) fusion(f32[512,2048]{1,0:T(8,128)} %copy-done.5, f32[2,2048]{1,0:T(2,128)S(1)} %subtract_divide_fusion, f32[512]{0:T(512)S(1)} %get-tuple-element.23, pred[512]{0:T(512)(128)(4,1)S(1)} %lt.30, f32[2048]{0:T(1024)S(1)} %copy-done.8), kind=kLoop, calls=%fused_computation.9 | loop fusion | flops 7337472 | bytes 4231680 | tf_op jit(solution)/shard_map/reduce_sum | solution.py:523
  73.2 1.3 %fusion.5 = bf16[512,2048]{1,0:T(8,128)(2,1)S(1)} fusion(f32[512,2048]{1,0:T(8,128)S(1)} %copy-done.6, f32[512]{0:T(512)S(1)} %broadcast_multiply_fusion, f32[512]{0:T(512)S(1)} %get-tuple-element.22, f32[2,2048]{1,0:T(2,128)S(1)} %subtract_divide_fusion, f32[2048]{0:T(1024)S(1)} %copy-done.8, f32[512]{0:T(512)S(1)} %get-tuple-element.23, ...), kind=kLoop, calls=%fused_computation.6 | loop fusion | flops 7340032 | bytes 6322688 | tf_op jit(solution)/shard_map/convert_element_type | solution.py:528
  74.5 0.9 copy-done.4
  75.4 3.4 %convolution_convert_fusion.1 = bf16[512,1024]{1,0:T(8,128)(2,1)} fusion(bf16[512,2048]{1,0:T(8,128)(2,1)S(1)} %fusion.5, bf16[1024,2048]{1,0:T(8,128)(2,1)S(1)} %copy-done.4), kind=kOutput, calls=%fused_computation.16 | convolution fusion | flops 2148007936 | bytes 7340032 | tf_op jit(solution)/shard_map/dot_general | solution.py:23
  78.7 2.4 %convert_bitcast_fusion.part_in = bf16[1024,2048]{1,0:T(8,128)(2,1)S(1)} fusion(bf16[512,2048]{1,0:T(8,128)(2,1)S(1)} %fusion.5, bf16[512,1024]{1,0:T(8,128)(2,1)S(1)} %copy-done), kind=kOutput, calls=%fused_computation.11 | convolution fusion | flops 2149580800 | bytes 7340032 | tf_op jit(solution)/shard_map/dot_general | solution.py:17
  81.2 38.7 %reduce_weight.1 = (bf16[128,2048]{1,0:T(8,128)(2,1)S(1)}, f32[32,1,2048]{2,1,0:T(1,128)S(1)}) custom-call(bf16[1024,2048]{1,0:T(8,128)(2,1)S(1)} %convert_bitcast_fusion.part_in, f32[1,2048]{1,0:T(1,128)S(1)} %bitcast.50), custom_call_target="tpu_custom_call" | custom-call | tf_op jit(solution)/shard_map/reduce_weight/pallas_call | solution.py:434
  119.9 0.8 reduce_sum.109
  120.6 0.8 copy.19
  (25 shorter events, 0.4 us)
Async XLA Ops:
  0.6 43.0 %copy-start = (bf16[512,1024]{1,0:T(8,128)(2,1)S(1)}, bf16[512,1024]{1,0:T(8,128)(2,1)}, u32[]{:S(2)}) copy-start(bf16[512,1024]{1,0:T(8,128)(2,1)} %param.9) | copy-start | bytes 3145732
  3.5 1.0 copy-start.1
  4.5 0.8 copy-start.2
  41.1 1.9 %copy-start.3 = (bf16[1024,2048]{1,0:T(8,128)(2,1)}, bf16[1024,2048]{1,0:T(8,128)(2,1)S(1)}, u32[]{:S(2)}) copy-start(bf16[1024,2048]{1,0:T(8,128)(2,1)S(1)} %get-tuple-element.13) | copy-start | bytes 12582916
  43.6 7.3 %copy-start.8 = (f32[2048]{0:T(1024)S(1)}, f32[2048]{0:T(1024)}, u32[]{:S(2)}) copy-start(f32[2048]{0:T(1024)} %param.12) | copy-start | bytes 24580
  49.0 2.0 %copy-start.5 = (f32[512,2048]{1,0:T(8,128)}, f32[512,2048]{1,0:T(8,128)S(1)}, u32[]{:S(2)}) copy-start(f32[512,2048]{1,0:T(8,128)S(1)} %get-tuple-element.27) | copy-start | bytes 12582916
  69.6 3.6 %copy-start.6 = (f32[512,2048]{1,0:T(8,128)S(1)}, f32[512,2048]{1,0:T(8,128)}, u32[]{:S(2)}) copy-start(f32[512,2048]{1,0:T(8,128)} %copy-done.5) | copy-start | bytes 12582916
  73.2 2.2 %copy-start.4 = (bf16[1024,2048]{1,0:T(8,128)(2,1)S(1)}, bf16[1024,2048]{1,0:T(8,128)(2,1)}, u32[]{:S(2)}) copy-start(bf16[1024,2048]{1,0:T(8,128)(2,1)} %copy-done.3) | copy-start | bytes 12582916
  75.4 3.4 %copy-start.7 = (bf16[512,2048]{1,0:T(8,128)(2,1)}, bf16[512,2048]{1,0:T(8,128)(2,1)S(1)}, u32[]{:S(2)}) copy-start(bf16[512,2048]{1,0:T(8,128)(2,1)S(1)} %fusion.5) | copy-start | bytes 6291460

commit v2 on v1

--- a/solution.py
+++ b/solution.py
@@ -68,12 +68,18 @@
 
 def gather_kernel(
     groups, ring, w_in, u_in, k_in, w_out, u_out, k_out,
-    own_sem, w_send, w_recv, p_send, p_recv, u_send, u_recv, k_send, k_recv,
-    du_send, du_recv, dk_send, dk_recv,
+    own_sem, w_send, w_recv, p_send, p_recv, y_send, y_recv,
+    u_send, u_recv, k_send, k_recv, ul_send, ul_recv, kl_send, kl_recv,
+    up_send, up_recv, kp_send, kp_recv,
 ):
     group, index = lax.axis_index("dp"), lax.axis_index("fsdp")
+    lines = groups // 2
+    split = lines == 2
+    slots = CHUNKS - 1 if split else CHUNKS
+    line = group // 2
     core = lax.rem(group, 2)
     partner = group + 1 - 2 * core
+    across = lax.rem(group + 2, groups)
     step = 1 - 2 * core
     place = ring_place(index, ring)
     rows = w_in.shape[0]
@@ -85,8 +91,13 @@
     def owner(s, way=step):
         return ring_index(lax.rem(place + ring * ring - s * way, ring), ring)
 
-    def w_slice(who, c, side=core):
-        start = pl.multiple_of(who * rows + side * half + c * part, part)
+    def chunk(j):
+        if not split or j < CHUNKS - 2:
+            return j
+        return CHUNKS - 2 + (line if j == CHUNKS - 2 else 1 - line)
+
+    def w_slice(who, j, side=core):
+        start = pl.multiple_of(who * rows + side * half + chunk(j) * part, part)
         return w_out.at[pl.ds(start, part), :]
 
     greet(
@@ -105,76 +116,117 @@
     for copy in own:
         copy.wait()
 
-    def w_ring(s, c):
-        ref = w_slice(owner(s), c)
-        return remote(ref, ref, w_send.at[s, c], w_recv.at[s, c], (group, following))
-
-    def w_ring_in(s, c):
-        ref = w_slice(owner(s + 1), c)
-        return remote(ref, ref, w_send.at[s, c], w_recv.at[s, c], (group, following))
-
-    def w_part(s, c):
-        ref = w_slice(owner(s + 1), c)
-        return remote(ref, ref, p_send.at[s, c], p_recv.at[s, c], (partner, index))
-
-    def w_part_in(s, c):
-        ref = w_slice(owner(s + 1, -step), c, 1 - core)
-        return remote(ref, ref, p_send.at[s, c], p_recv.at[s, c], (partner, index))
-
-    small = ((u_out, u_send, u_recv, du_send, du_recv), (k_out, k_send, k_recv, dk_send, dk_recv))
+    def w_ring(s, j, shift=0):
+        ref = w_slice(owner(s + shift), j)
+        return remote(ref, ref, w_send.at[s, j], w_recv.at[s, j], (group, following))
+
+    def w_part(s, j):
+        ref = w_slice(owner(s + 1), j)
+        return remote(ref, ref, p_send.at[s, j], p_recv.at[s, j], (partner, index))
+
+    def w_part_in(s, j):
+        ref = w_slice(owner(s + 1, -step), j, 1 - core)
+        return remote(ref, ref, p_send.at[s, j], p_recv.at[s, j], (partner, index))
+
+    def w_across(s, j):
+        ref = w_slice(owner(s + 1), j)
+        return remote(ref, ref, y_send.at[s], y_recv.at[s], (across, index))
+
+    small = (
+        (u_out, u_send, u_recv, ul_send, ul_recv, up_send, up_recv),
+        (k_out, k_send, k_recv, kl_send, kl_recv, kp_send, kp_recv),
+    )
 
     def s_ring(a, s, shift):
-        out, send, recv, _, _ = small[a]
+        out, send, recv = small[a][:3]
         ref = out.at[group * ring + owner(s + shift)]
         return remote(ref, ref, send.at[s], recv.at[s], (group, following))
 
-    def s_out(a, s, k):
-        out, _, _, send, recv = small[a]
+    def s_line(a, s, k):
+        out, _, _, send, recv = small[a][:5]
         ref = out.at[group * ring + owner(s)]
-        peer = lax.rem(group + k, groups)
+        peer = lax.rem(group + 2 * k, groups)
         return remote(ref, ref, send.at[s, k - 1], recv.at[s, k - 1], (peer, index))
 
-    def s_in(a, s, k):
-        out, _, _, send, recv = small[a]
-        source = lax.rem(group + groups - k, groups)
-        way = 1 - 2 * lax.rem(source, 2)
-        ref = out.at[source * ring + owner(s, way)]
+    def s_line_in(a, s, k):
+        out, _, _, send, recv = small[a][:5]
+        source = lax.rem(group + groups - 2 * k, groups)
+        ref = out.at[source * ring + owner(s)]
         return remote(ref, ref, send.at[s, k - 1], recv.at[s, k - 1], (source, index))
 
-    for c in range(CHUNKS):
-        w_ring(0, c).start()
+    def s_part(a, s, k):
+        out, send, recv = small[a][0], small[a][5], small[a][6]
+        source = lax.rem(group + groups - 2 * k, groups)
+        ref = out.at[source * ring + owner(s)]
+        return remote(ref, ref, send.at[s, k], recv.at[s, k], (partner, index))
+
+    def s_part_in(a, s, k):
+        out, send, recv = small[a][0], small[a][5], small[a][6]
+        source = lax.rem(partner + groups - 2 * k, groups)
+        ref = out.at[source * ring + owner(s, -step)]
+        return remote(ref, ref, send.at[s, k], recv.at[s, k], (partner, index))
+
+    def w_pass(s):
+        if split:
+            w_across(s, CHUNKS - 1).wait_recv()
+            w_part(s, CHUNKS - 1).start()
+
+    def spread(s):
+        for a in (0, 1):
+            for k in range(1, lines):
+                s_line(a, s, k).start()
+            s_part(a, s, 0).start()
+
+    def s_pass(s):
+        for a in (0, 1):
+            for k in range(1, lines):
+                s_line_in(a, s, k).wait_recv()
+                s_part(a, s, k).start()
+
+    def receive(s, more):
+        for j in range(slots):
+            w_ring(s - 1, j, 1).wait_recv()
+            if more:
+                w_ring(s, j).start()
+            if split and j == CHUNKS - 2:
+                w_across(s - 1, j).start()
+            w_part(s - 1, j).start()
+        for a in (0, 1):
+            s_ring(a, s - 1, 1).wait_recv()
+            if more:
+                s_ring(a, s, 0).start()
+        spread(s)
+
+    for j in range(slots):
+        w_ring(0, j).start()
     for a in (0, 1):
         s_ring(a, 0, 0).start()
-        for k in range(1, groups):
-            s_out(a, 0, k).start()
+    spread(0)
+    receive(1, True)
+    s_pass(0)
 
     def forward(s, carry):
-        for c in range(CHUNKS):
-            w_ring_in(s - 1, c).wait_recv()
-            w_ring(s, c).start()
-            w_part(s - 1, c).start()
-        for a in (0, 1):
-            s_ring(a, s - 1, 1).wait_recv()
-            s_ring(a, s, 0).start()
-            for k in range(1, groups):
-                s_out(a, s, k).start()
-        return carry
-
-    lax.fori_loop(1, ring - 1, forward, 0)
+        receive(s, True)
+        w_pass(s - 2)
+        s_pass(s - 1)
+        return carry
+
+    lax.fori_loop(2, ring - 1, forward, 0)
     last = ring - 1
-    for c in range(CHUNKS):
-        w_ring_in(last - 1, c).wait_recv()
-        w_part(last - 1, c).start()
-    for a in (0, 1):
-        s_ring(a, last - 1, 1).wait_recv()
-        for k in range(1, groups):
-            s_out(a, last, k).start()
+    receive(last, False)
+    w_pass(last - 2)
+    s_pass(last - 1)
+    w_pass(last - 1)
+    s_pass(last)
 
     def finish(s, carry):
-        for c in range(CHUNKS):
-            w_ring(s, c).wait_send()
-            w_part(s, c).wait_send()
-            w_part_in(s, c).wait_recv()
+        for j in range(slots):
+            w_ring(s, j).wait_send()
+        if split:
+            w_across(s, CHUNKS - 2).wait_send()
+        for j in range(CHUNKS):
+            w_part(s, j).wait_send()
+            w_part_in(s, j).wait_recv()
         for a in (0, 1):
             s_ring(a, s, 0).wait_send()
         return carry
@@ -183,9 +235,11 @@
 
     def finish_small(s, carry):
         for a in (0, 1):
-            for k in range(1, groups):
-                s_out(a, s, k).wait_send()
-                s_in(a, s, k).wait_recv()
+            for k in range(1, lines):
+                s_line(a, s, k).wait_send()
+            for k in range(lines):
+                s_part(a, s, k).wait_send()
+                s_part_in(a, s, k).wait_recv()
         return carry
 
     lax.fori_loop(0, ring, finish_small, 0)
@@ -193,6 +247,7 @@
 
 def gather_inputs(groups, ring, weight, users, keys):
     total = groups * ring
+    lines = groups // 2
     rows, width = weight.shape
     dma = pltpu.SemaphoreType.DMA
     vmem = pl.BlockSpec(memory_space=pltpu.VMEM)
@@ -208,8 +263,10 @@
         out_specs=(vmem, vmem, vmem),
         scratch_shapes=[dma((3,))]
         + [dma((ring - 1, CHUNKS))] * 4
+        + [dma((ring - 1,))] * 2
         + [dma((ring - 1,))] * 4
-        + [dma((ring, groups - 1))] * 4,
+        + [dma((ring, max(lines - 1, 1)))] * 4
+        + [dma((ring, lines))] * 4,
         compiler_params=pltpu.CompilerParams(
             collective_id=0, has_side_effects=True, vmem_limit_bytes=32 << 20
         ),
@@ -269,8 +326,9 @@
 
 def reduce_kernel(
     groups, ring, part_in, gain_in, out, gain_out,
-    cross, held, arrived, totals,
+    cross, held, arrived, totals, lent, borrowed,
     own_sem, g_send, g_recv, x_send, x_recv, r_send, r_recv, t_send, t_recv, o_send, o_recv,
+    y_send, y_recv, f_send, f_recv,
 ):
     total = groups * ring
     group, index = lax.axis_index("dp"), lax.axis_index("fsdp")
@@ -284,10 +342,18 @@
     piece = half // CHUNKS
     lines = groups // 2
     line = group // 2
+    split = lines == 2
+    slots = CHUNKS - 1 if split else CHUNKS
+    across = lax.rem(group + 2, groups)
     following = ring_index(lax.rem(place + ring + step, ring), ring)
 
     def owner(s, way=step):
         return ring_index(lax.rem(place + ring * ring - (s + 1) * way, ring), ring)
+
+    def chunk(j):
+        if not split or j < CHUNKS - 2:
+            return j
+        return CHUNKS - 2 + (line if j == CHUNKS - 2 else 1 - line)
 
     greet_all(groups, ring, me)
 
@@ -334,79 +400,111 @@
             (group, following),
         )
 
-    def local_term(s, c):
-        start = pl.multiple_of(owner(s) * rows + core * half + c * piece, piece)
+    def local_term(s, j):
+        offset = chunk(j) * piece
+        start = pl.multiple_of(owner(s) * rows + core * half + offset, piece)
         mine = part_in[pl.ds(start, piece), :].astype(jnp.float32)
-        return mine + cross[s, pl.ds(c * piece, piece), :].astype(jnp.float32)
-
-    cross_out(0).wait_recv()
-    for c in range(CHUNKS):
-        held[0, pl.ds(c * piece, piece), :] = local_term(0, c).astype(held.dtype)
-        ring_copy(0, c).start()
+        return mine + cross[s, pl.ds(pl.multiple_of(offset, piece), piece), :].astype(jnp.float32)
+
+    def lend(s):
+        return remote(lent.at[s], borrowed.at[s], y_send.at[s], y_recv.at[s], (across, index))
+
+    def prepare(s):
+        cross_out(s).wait_recv()
+        if split:
+            lent[s] = local_term(s, CHUNKS - 1).astype(lent.dtype)
+            lend(s).start()
+
+    def term_of(s, j):
+        term = local_term(s, j)
+        if split and j == CHUNKS - 2:
+            lend(s).wait_recv()
+            term = term + borrowed[s].astype(jnp.float32)
+        return term
+
+    prepare(0)
+    for j in range(slots):
+        if j == CHUNKS - 2:
+            prepare(1)
+        held[0, pl.ds(j * piece, piece), :] = term_of(0, j).astype(held.dtype)
+        ring_copy(0, j).start()
 
     def pass_on(s, carry):
-        cross_out(s).wait_recv()
-        for c in range(CHUNKS):
-            at = pl.ds(c * piece, piece)
-            term = local_term(s, c)
-            ring_copy(s - 1, c).wait_recv()
+        for j in range(slots):
+            at = pl.ds(j * piece, piece)
+            if j == CHUNKS - 2:
+                prepare(s + 1)
+            term = term_of(s, j)
+            ring_copy(s - 1, j).wait_recv()
             held[s, at, :] = (term + arrived[s - 1, at, :].astype(jnp.float32)).astype(held.dtype)
-            ring_copy(s, c).start()
+            ring_copy(s, j).start()
         return carry
 
     lax.fori_loop(1, ring - 1, pass_on, 0)
     last = ring - 1
-    cross_out(last).wait_recv()
-
-    def total_copy(k, c):
-        at = pl.ds(c * piece, piece)
-        ref = totals.at[line, at, :]
+
+    def total_copy(k, j):
+        ref = totals.at[line, pl.ds(j * piece, piece), :]
         return remote(
-            ref, ref, t_send.at[k - 1, c], t_recv.at[k - 1, c],
+            ref, ref, t_send.at[k - 1, j], t_recv.at[k - 1, j],
             (lax.rem(group + 2 * k, groups), index),
         )
 
-    def total_in(k, c):
-        at = pl.ds(c * piece, piece)
+    def total_in(k, j):
         source = lax.rem(group + groups - 2 * k, groups)
-        ref = totals.at[source // 2, at, :]
-        return remote(ref, ref, t_send.at[k - 1, c], t_recv.at[k - 1, c], (source, index))
-
-    for c in range(CHUNKS):
-        at = pl.ds(c * piece, piece)
-        term = local_term(last, c)
-        ring_copy(last - 1, c).wait_recv()
-        totals[line, at, :] = (term + arrived[last - 1, at, :].astype(jnp.float32)).astype(
-            totals.dtype
-        )
+        ref = totals.at[source // 2, pl.ds(j * piece, piece), :]
+        return remote(ref, ref, t_send.at[k - 1, j], t_recv.at[k - 1, j], (source, index))
+
+    def out_rows(j, side=core):
+        return pl.ds(pl.multiple_of(side * half + chunk(j) * piece, piece), piece)
+
+    def out_copy(j, side):
+        ref = out.at[out_rows(j, side), :]
+        return remote(ref, ref, o_send.at[j], o_recv.at[j], (partner, index))
+
+    def out_across(j):
+        ref = out.at[out_rows(j), :]
+        return remote(ref, ref, f_send.at[0], f_recv.at[0], (across, index))
+
+    shared = range(CHUNKS - 2) if split else range(CHUNKS)
+    for j in range(slots):
+        at = pl.ds(j * piece, piece)
+        term = term_of(last, j)
+        ring_copy(last - 1, j).wait_recv()
+        value = (term + arrived[last - 1, at, :].astype(jnp.float32)).astype(totals.dtype)
+        if j in shared:
+            totals[line, at, :] = value
+            for k in range(1, lines):
+                total_copy(k, j).start()
+        else:
+            out[out_rows(j), :] = value
+            out_across(j).start()
+            out_copy(j, core).start()
+
+    for j in shared:
+        at = pl.ds(j * piece, piece)
         for k in range(1, lines):
-            total_copy(k, c).start()
-
-    def out_copy(c, side):
-        ref = out.at[pl.ds(pl.multiple_of(side * half + c * piece, piece), piece), :]
-        return remote(ref, ref, o_send.at[c], o_recv.at[c], (partner, index))
-
-    for c in range(CHUNKS):
-        at = pl.ds(c * piece, piece)
-        for k in range(1, lines):
-            total_in(k, c).wait_recv()
+            total_in(k, j).wait_recv()
         value = totals[0, at, :].astype(jnp.float32)
-        for j in range(1, lines):
-            value = value + totals[j, at, :].astype(jnp.float32)
-        out[pl.ds(pl.multiple_of(core * half + c * piece, piece), piece), :] = value.astype(
-            out.dtype
-        )
-        out_copy(c, core).start()
+        for other in range(1, lines):
+            value = value + totals[other, at, :].astype(jnp.float32)
+        out[out_rows(j), :] = value.astype(out.dtype)
+        out_copy(j, core).start()
+    if split:
+        out_across(CHUNKS - 1).wait_recv()
+        out_copy(CHUNKS - 1, core).start()
 
     def finish_cross(s, carry):
         cross_out(s).wait_send()
+        if split:
+            lend(s).wait_send()
         return carry
 
     lax.fori_loop(0, ring, finish_cross, 0)
 
     def finish_ring(s, carry):
-        for c in range(CHUNKS):
-            ring_copy(s, c).wait_send()
+        for j in range(slots):
+            ring_copy(s, j).wait_send()
         return carry
 
     lax.fori_loop(0, ring - 1, finish_ring, 0)
@@ -418,11 +516,14 @@
         return carry
 
     lax.fori_loop(1, total, finish_gain, 0)
-    for c in range(CHUNKS):
+    for j in shared:
         for k in range(1, lines):
-            total_copy(k, c).wait_send()
-        out_copy(c, core).wait_send()
-        out_copy(c, 1 - core).wait_recv()
+            total_copy(k, j).wait_send()
+    for j in range(CHUNKS):
+        out_copy(j, core).wait_send()
+        out_copy(j, 1 - core).wait_recv()
+    if split:
+        out_across(CHUNKS - 2).wait_send()
 
 
 def reduce_weight(groups, ring, partial, gain):
@@ -444,6 +545,8 @@
             pltpu.VMEM((ring - 1, half, width), partial.dtype),
             pltpu.VMEM((ring - 1, half, width), partial.dtype),
             pltpu.VMEM((groups // 2, half, width), partial.dtype),
+            pltpu.VMEM((ring, half // CHUNKS, width), partial.dtype),
+            pltpu.VMEM((ring, half // CHUNKS, width), partial.dtype),
             dma,
             dma((total - 1,)),
             dma((total - 1,)),
@@ -451,10 +554,14 @@
             dma((ring,)),
             dma((ring - 1, CHUNKS)),
             dma((ring - 1, CHUNKS)),
-            dma((groups // 2 - 1, CHUNKS)),
-            dma((groups // 2 - 1, CHUNKS)),
+            dma((max(groups // 2 - 1, 1), CHUNKS)),
+            dma((max(groups // 2 - 1, 1), CHUNKS)),
             dma((CHUNKS,)),
             dma((CHUNKS,)),
+            dma((ring,)),
+            dma((ring,)),
+            dma((1,)),
+            dma((1,)),
         ],
         compiler_params=pltpu.CompilerParams(
             collective_id=2, has_side_effects=True, vmem_limit_bytes=40 << 20

time: 123 us -> 123 us (level)
  no operation moved by 1% of the time
where the time goes in v2:
time: 123 us; the launch traced here: 122 us
  Pallas kernels  87 us (71%)
  matrix products  12.8 us (10%)
  local copies, waits for them, and re-layouts  10.2 us (8%)
  other arithmetic  9.67 us (8%)
  between operations  2.61 us (2%)
    pallas_call x1, Pallas kernels, reduce_weight(): pl.pallas_call(functools.partial(reduce_kernel, groups, ring), out_shape=...  38.6 us
    pallas_call x1, Pallas kernels, gather_inputs(): pl.pallas_call(functools.partial(gather_kernel, groups, ring), out_shape=...  35.3 us
    pallas_call x1, Pallas kernels, share(): pl.pallas_call(functools.partial(share_kernel, groups, ring), out_shape=j...  13.1 us
    unnamed x19, local copies, waits for them, and re-layouts  7.36 us
    dot_general x1, matrix products, on_device(): attended = jnp.dot(context, weight_all, preferred_element_type=jnp.float32)  5.35 us
    dot_general x2, matrix products, contract_last(): lax.dot_general(left, right, (((1,), (1,)), ((), ())), preferred_element_...  3.82 us
    reduce_sum x1, other arithmetic, on_device(): gain_part = jnp.sum(normed_grad * stream * inverse_root_mean, axis=0)  3.5 us
    dot_general x2, matrix products, contract_rows(): lax.dot_general(left, right, (((0,), (0,)), ((), ())), preferred_element_...  2.79 us

profile of v2, /device:TPU:0, one launch (start us, length us, event | category | flops | bytes accessed | tf_op | source)
XLA Modules:
  0.0 122.2 jit_solution(6289322230311396649)
XLA Ops:
  0.7 0.7 convert_element_type.38
  1.4 0.7 pad_bitcast_fusion.2
  2.1 0.7 iota_compare_fusion.1
  2.8 0.7 pad_bitcast_fusion
  3.5 1.0 copy-done.1
  4.5 0.8 copy-done.2
  5.3 35.3 %gather_inputs.1 = (bf16[1024,2048]{1,0:T(8,128)(2,1)S(1)}, bf16[32,8,2048]{2,1,0:T(8,128)(2,1)S(1)}, s32[32,8,128]{2,1,0:T(8,128)S(1)}) custom-call(bf16[128,2048]{1,0:T(8,128)(2,1)S(1)} %copy-done.1, bf16[8,2048]{1,0:T(8,128)(2,1)S(1)} %copy-done.2, s32[8,128]{1,0:T(8,128)S(1)} %pad.18.k_in), custom_call_target="tpu_custom_call" | custom-call | tf_op jit(solution)/shard_map/gather_inputs/pallas_call | solution.py:255
  40.6 1.9 %copy-done.3 = bf16[1024,2048]{1,0:T(8,128)(2,1)} copy-done((bf16[1024,2048]{1,0:T(8,128)(2,1)}, bf16[1024,2048]{1,0:T(8,128)(2,1)S(1)}, u32[]{:S(2)}) %copy-start.3) | copy-done | bytes 4194328
  42.6 0.1 log.14
  42.8 0.1 eq.30
  43.0 0.1 select_reduce_fusion.2
  43.1 5.3 %multiply_reduce_fusion = (f32[512]{0:T(512)S(1)}, f32[512,2048]{1,0:T(8,128)S(1)}) fusion(bf16[512,1024]{1,0:T(8,128)(2,1)S(1)} %copy-done, bf16[1024,2048]{1,0:T(8,128)(2,1)} %copy-done.3, bf16[512,2048]{1,0:T(8,128)(2,1)} %param.10), kind=kOutput, calls=%fused_computation.14 | convolution fusion | flops 2151677440 | bytes 11536384 | tf_op jit(solution)/shard_map/dot_general | solution.py:593
  48.5 2.0 %copy-done.5 = f32[512,2048]{1,0:T(8,128)} copy-done((f32[512,2048]{1,0:T(8,128)}, f32[512,2048]{1,0:T(8,128)S(1)}, u32[]{:S(2)}) %copy-start.5) | copy-done | bytes 4194328
  50.4 0.7 select_reduce_fusion
  51.1 0.2 multiply_reduce_fusion.2
  51.4 0.7 multiply_convert_fusion.x_in
  52.0 13.1 %share.1 = bf16[32,2,2048]{2,1,0:T(2,128)(2,1)} custom-call(bf16[2,2048]{1,0:T(2,128)(2,1)} %multiply_convert_fusion.x_in), custom_call_target="tpu_custom_call" | custom-call | tf_op jit(solution)/shard_map/share/pallas_call | solution.py:316
  65.2 1.0 reshape.107
  66.2 0.5 fusion.20
  66.7 0.1 fusion.15
  66.8 0.1 subtract_convert_fusion
  66.9 0.4 multiply_reduce_fusion.1
  67.2 0.9 convolution_convert_fusion
  68.1 0.6 subtract_reduce_fusion
  69.5 3.5 %fusion.8 = (f32[2048]{0:T(1024)S(1)}, f32[512]{0:T(512)S(1)}) fusion(f32[512,2048]{1,0:T(8,128)} %copy-done.5, f32[2,2048]{1,0:T(2,128)S(1)} %subtract_divide_fusion, f32[512]{0:T(512)S(1)} %get-tuple-element.23, pred[512]{0:T(512)(128)(4,1)S(1)} %lt.30, f32[2048]{0:T(1024)S(1)} %copy-done.8), kind=kLoop, calls=%fused_computation.9 | loop fusion | flops 7337472 | bytes 4231680 | tf_op jit(solution)/shard_map/reduce_sum | solution.py:630
  73.0 1.3 %fusion.5 = bf16[512,2048]{1,0:T(8,128)(2,1)S(1)} fusion(f32[512,2048]{1,0:T(8,128)S(1)} %copy-done.6, f32[512]{0:T(512)S(1)} %broadcast_multiply_fusion, f32[512]{0:T(512)S(1)} %get-tuple-element.22, f32[2,2048]{1,0:T(2,128)S(1)} %subtract_divide_fusion, f32[2048]{0:T(1024)S(1)} %copy-done.8, f32[512]{0:T(512)S(1)} %get-tuple-element.23, ...), kind=kLoop, calls=%fused_computation.6 | loop fusion | flops 7340032 | bytes 6322688 | tf_op jit(solution)/shard_map/convert_element_type | solution.py:635
  74.3 0.9 copy-done.4
  75.2 3.4 %convolution_convert_fusion.1 = bf16[512,1024]{1,0:T(8,128)(2,1)} fusion(bf16[512,2048]{1,0:T(8,128)(2,1)S(1)} %fusion.5, bf16[1024,2048]{1,0:T(8,128)(2,1)S(1)} %copy-done.4), kind=kOutput, calls=%fused_computation.16 | convolution fusion | flops 2148007936 | bytes 7340032 | tf_op jit(solution)/shard_map/dot_general | solution.py:23
  78.6 2.4 %convert_bitcast_fusion.part_in = bf16[1024,2048]{1,0:T(8,128)(2,1)S(1)} fusion(bf16[512,2048]{1,0:T(8,128)(2,1)S(1)} %fusion.5, bf16[512,1024]{1,0:T(8,128)(2,1)S(1)} %copy-done), kind=kOutput, calls=%fused_computation.11 | convolution fusion | flops 2149580800 | bytes 7340032 | tf_op jit(solution)/shard_map/dot_general | solution.py:17
  81.0 38.6 %reduce_weight.1 = (bf16[128,2048]{1,0:T(8,128)(2,1)S(1)}, f32[32,1,2048]{2,1,0:T(1,128)S(1)}) custom-call(bf16[1024,2048]{1,0:T(8,128)(2,1)S(1)} %convert_bitcast_fusion.part_in, f32[1,2048]{1,0:T(1,128)S(1)} %bitcast.50), custom_call_target="tpu_custom_call" | custom-call | tf_op jit(solution)/shard_map/reduce_weight/pallas_call | solution.py:535
  119.5 0.8 reduce_sum.109
  120.3 0.8 copy.19
  (25 shorter events, 0.4 us)
Async XLA Ops:
  0.6 42.5 %copy-start = (bf16[512,1024]{1,0:T(8,128)(2,1)S(1)}, bf16[512,1024]{1,0:T(8,128)(2,1)}, u32[]{:S(2)}) copy-start(bf16[512,1024]{1,0:T(8,128)(2,1)} %param.9) | copy-start | bytes 3145732
  3.5 1.0 copy-start.1
  4.5 0.8 copy-start.2
  40.6 1.9 %copy-start.3 = (bf16[1024,2048]{1,0:T(8,128)(2,1)}, bf16[1024,2048]{1,0:T(8,128)(2,1)S(1)}, u32[]{:S(2)}) copy-start(bf16[1024,2048]{1,0:T(8,128)(2,1)S(1)} %get-tuple-element.13) | copy-start | bytes 12582916
  43.1 7.3 %copy-start.8 = (f32[2048]{0:T(1024)S(1)}, f32[2048]{0:T(1024)}, u32[]{:S(2)}) copy-start(f32[2048]{0:T(1024)} %param.12) | copy-start | bytes 24580
  48.5 2.0 %copy-start.5 = (f32[512,2048]{1,0:T(8,128)}, f32[512,2048]{1,0:T(8,128)S(1)}, u32[]{:S(2)}) copy-start(f32[512,2048]{1,0:T(8,128)S(1)} %get-tuple-element.27) | copy-start | bytes 12582916
  69.4 3.6 %copy-start.6 = (f32[512,2048]{1,0:T(8,128)S(1)}, f32[512,2048]{1,0:T(8,128)}, u32[]{:S(2)}) copy-start(f32[512,2048]{1,0:T(8,128)} %copy-done.5) | copy-start | bytes 12582916
  73.0 2.2 %copy-start.4 = (bf16[1024,2048]{1,0:T(8,128)(2,1)S(1)}, bf16[1024,2048]{1,0:T(8,128)(2,1)}, u32[]{:S(2)}) copy-start(bf16[1024,2048]{1,0:T(8,128)(2,1)} %copy-done.3) | copy-start | bytes 12582916
  75.2 3.4 %copy-start.7 = (bf16[512,2048]{1,0:T(8,128)(2,1)}, bf16[512,2048]{1,0:T(8,128)(2,1)S(1)}, u32[]{:S(2)}) copy-start(bf16[512,2048]{1,0:T(8,128)(2,1)S(1)} %fusion.5) | copy-start | bytes 6291460

commit v3 on v2

--- a/solution.py
+++ b/solution.py
@@ -80,16 +80,21 @@
     core = lax.rem(group, 2)
     partner = group + 1 - 2 * core
     across = lax.rem(group + 2, groups)
-    step = 1 - 2 * core
     place = ring_place(index, ring)
+    ends = (
+        ring_index(lax.rem(place + 1, ring), ring),
+        ring_index(lax.rem(place + ring - 1, ring), ring),
+    )
     rows = w_in.shape[0]
     half = rows // 2
     part = half // CHUNKS
-    following = ring_index(lax.rem(place + ring + step, ring), ring)
-    previous = ring_index(lax.rem(place + ring - step, ring), ring)
-
-    def owner(s, way=step):
-        return ring_index(lax.rem(place + ring * ring - s * way, ring), ring)
+    hops = ring - 1
+
+    def owner(m):
+        if m == hops + 2:
+            return index
+        away = -(m // 2) if m % 2 == 0 else m // 2
+        return ring_index(lax.rem(place + ring + away, ring), ring)
 
     def chunk(j):
         if not split or j < CHUNKS - 2:
@@ -102,7 +107,7 @@
 
     greet(
         [(lax.rem(group + k, groups), index) for k in range(1, groups)]
-        + [(group, following), (group, previous)]
+        + [(group, end) for end in ends]
     )
     own = [
         pltpu.make_async_copy(
@@ -116,54 +121,50 @@
     for copy in own:
         copy.wait()
 
-    def w_ring(s, j, shift=0):
-        ref = w_slice(owner(s + shift), j)
-        return remote(ref, ref, w_send.at[s, j], w_recv.at[s, j], (group, following))
-
-    def w_part(s, j):
-        ref = w_slice(owner(s + 1), j)
-        return remote(ref, ref, p_send.at[s, j], p_recv.at[s, j], (partner, index))
-
-    def w_part_in(s, j):
-        ref = w_slice(owner(s + 1, -step), j, 1 - core)
-        return remote(ref, ref, p_send.at[s, j], p_recv.at[s, j], (partner, index))
-
-    def w_across(s, j):
-        ref = w_slice(owner(s + 1), j)
-        return remote(ref, ref, y_send.at[s], y_recv.at[s], (across, index))
+    def w_ring(m, j, shift=0):
+        ref = w_slice(owner(m + shift), j)
+        return remote(ref, ref, w_send.at[m, j], w_recv.at[m, j], (group, ends[m % 2]))
+
+    def w_part(m, j, side=core):
+        ref = w_slice(owner(m + 2), j, side)
+        return remote(ref, ref, p_send.at[m, j], p_recv.at[m, j], (partner, index))
+
+    def w_across(m, j):
+        ref = w_slice(owner(m + 2), j)
+        return remote(ref, ref, y_send.at[m], y_recv.at[m], (across, index))
 
     small = (
         (u_out, u_send, u_recv, ul_send, ul_recv, up_send, up_recv),
         (k_out, k_send, k_recv, kl_send, kl_recv, kp_send, kp_recv),
     )
 
-    def s_ring(a, s, shift):
+    def s_ring(a, m, shift):
         out, send, recv = small[a][:3]
-        ref = out.at[group * ring + owner(s + shift)]
-        return remote(ref, ref, send.at[s], recv.at[s], (group, following))
+        ref = out.at[group * ring + owner(m + shift)]
+        return remote(ref, ref, send.at[m], recv.at[m], (group, ends[m % 2]))
 
     def s_line(a, s, k):
         out, _, _, send, recv = small[a][:5]
-        ref = out.at[group * ring + owner(s)]
+        ref = out.at[group * ring + owner(s + 2)]
         peer = lax.rem(group + 2 * k, groups)
         return remote(ref, ref, send.at[s, k - 1], recv.at[s, k - 1], (peer, index))
 
     def s_line_in(a, s, k):
         out, _, _, send, recv = small[a][:5]
         source = lax.rem(group + groups - 2 * k, groups)
-        ref = out.at[source * ring + owner(s)]
+        ref = out.at[source * ring + owner(s + 2)]
         return remote(ref, ref, send.at[s, k - 1], recv.at[s, k - 1], (source, index))
 
     def s_part(a, s, k):
         out, send, recv = small[a][0], small[a][5], small[a][6]
         source = lax.rem(group + groups - 2 * k, groups)
-        ref = out.at[source * ring + owner(s)]
+        ref = out.at[source * ring + owner(s + 2)]
         return remote(ref, ref, send.at[s, k], recv.at[s, k], (partner, index))
 
     def s_part_in(a, s, k):
         out, send, recv = small[a][0], small[a][5], small[a][6]
         source = lax.rem(partner + groups - 2 * k, groups)
-        ref = out.at[source * ring + owner(s, -step)]
+        ref = out.at[source * ring + owner(s + 2)]
         return remote(ref, ref, send.at[s, k], recv.at[s, k], (partner, index))
 
     def w_pass(s):
@@ -183,66 +184,52 @@
                 s_line_in(a, s, k).wait_recv()
                 s_part(a, s, k).start()
 
-    def receive(s, more):
+    for m in range(min(2, hops)):
         for j in range(slots):
-            w_ring(s - 1, j, 1).wait_recv()
+            w_ring(m, j).start()
+    for m in range(min(2, hops)):
+        for a in (0, 1):
+            s_ring(a, m, 0).start()
+    spread(hops)
+    for m in range(hops):
+        more = m + 2 < hops
+        for j in range(slots):
+            w_ring(m, j, 2).wait_recv()
             if more:
-                w_ring(s, j).start()
+                w_ring(m + 2, j).start()
             if split and j == CHUNKS - 2:
-                w_across(s - 1, j).start()
-            w_part(s - 1, j).start()
+                w_across(m, j).start()
+            w_part(m, j).start()
         for a in (0, 1):
-            s_ring(a, s - 1, 1).wait_recv()
+            s_ring(a, m, 2).wait_recv()
             if more:
-                s_ring(a, s, 0).start()
-        spread(s)
-
-    for j in range(slots):
-        w_ring(0, j).start()
-    for a in (0, 1):
-        s_ring(a, 0, 0).start()
-    spread(0)
-    receive(1, True)
-    s_pass(0)
-
-    def forward(s, carry):
-        receive(s, True)
-        w_pass(s - 2)
-        s_pass(s - 1)
-        return carry
-
-    lax.fori_loop(2, ring - 1, forward, 0)
-    last = ring - 1
-    receive(last, False)
-    w_pass(last - 2)
-    s_pass(last - 1)
-    w_pass(last - 1)
-    s_pass(last)
-
-    def finish(s, carry):
+                s_ring(a, m + 2, 0).start()
+        spread(m)
+        if m == 1:
+            s_pass(hops)
+        if m >= 2:
+            w_pass(m - 2)
+            s_pass(m - 2)
+    for m in range(hops - 2, hops):
+        w_pass(m)
+        s_pass(m)
+    for m in range(hops):
         for j in range(slots):
-            w_ring(s, j).wait_send()
+            w_ring(m, j).wait_send()
         if split:
-            w_across(s, CHUNKS - 2).wait_send()
+            w_across(m, CHUNKS - 2).wait_send()
         for j in range(CHUNKS):
-            w_part(s, j).wait_send()
-            w_part_in(s, j).wait_recv()
+            w_part(m, j).wait_send()
+            w_part(m, j, 1 - core).wait_recv()
         for a in (0, 1):
-            s_ring(a, s, 0).wait_send()
-        return carry
-
-    lax.fori_loop(0, ring - 1, finish, 0)
-
-    def finish_small(s, carry):
+            s_ring(a, m, 0).wait_send()
+    for m in range(ring):
         for a in (0, 1):
             for k in range(1, lines):
-                s_line(a, s, k).wait_send()
+                s_line(a, m, k).wait_send()
             for k in range(lines):
-                s_part(a, s, k).wait_send()
-                s_part_in(a, s, k).wait_recv()
-        return carry
-
-    lax.fori_loop(0, ring, finish_small, 0)
+                s_part(a, m, k).wait_send()
+                s_part_in(a, m, k).wait_recv()
 
 
 def gather_inputs(groups, ring, weight, users, keys):
@@ -335,8 +322,12 @@
     me = group * ring + index
     core = lax.rem(group, 2)
     partner = group + 1 - 2 * core
-    step = 1 - 2 * core
     place = ring_place(index, ring)
+    ends = (
+        ring_index(lax.rem(place + 1, ring), ring),
+        ring_index(lax.rem(place + ring - 1, ring), ring),
+    )
+    hops = ring - 1
     rows = part_in.shape[0] // ring
     half = rows // 2
     piece = half // CHUNKS
@@ -345,10 +336,12 @@
     split = lines == 2
     slots = CHUNKS - 1 if split else CHUNKS
     across = lax.rem(group + 2, groups)
-    following = ring_index(lax.rem(place + ring + step, ring), ring)
-
-    def owner(s, way=step):
-        return ring_index(lax.rem(place + ring * ring - (s + 1) * way, ring), ring)
+
+    def owner(m):
+        if m == hops:
+            return index
+        away = ring // 2 - m // 2 if m % 2 == 0 else m // 2 - (ring - 1) // 2
+        return ring_index(lax.rem(place + ring + away, ring), ring)
 
     def chunk(j):
         if not split or j < CHUNKS - 2:
@@ -357,19 +350,15 @@
 
     greet_all(groups, ring, me)
 
-    def cross_out(s):
-        who = owner(s, -step)
-        start = pl.multiple_of(who * rows + (1 - core) * half, half)
+    def cross_out(m):
+        start = pl.multiple_of(owner(m) * rows + (1 - core) * half, half)
         return remote(
-            part_in.at[pl.ds(start, half), :], cross.at[s], x_send.at[s], x_recv.at[s],
+            part_in.at[pl.ds(start, half), :], cross.at[m], x_send.at[m], x_recv.at[m],
             (partner, index),
         )
 
-    def start_cross(s, carry):
-        cross_out(s).start()
-        return carry
-
-    lax.fori_loop(0, ring, start_cross, 0)
+    for m in range(ring):
+        cross_out(m).start()
 
     def gain_push(k):
         peer = lax.rem(me + k, total)
@@ -397,7 +386,7 @@
         at = pl.ds(c * piece, piece)
         return remote(
             held.at[s, at, :], arrived.at[s, at, :], r_send.at[s, c], r_recv.at[s, c],
-            (group, following),
+            (group, ends[s % 2]),
         )
 
     def local_term(s, j):
@@ -422,26 +411,20 @@
             term = term + borrowed[s].astype(jnp.float32)
         return term
 
-    prepare(0)
-    for j in range(slots):
-        if j == CHUNKS - 2:
-            prepare(1)
-        held[0, pl.ds(j * piece, piece), :] = term_of(0, j).astype(held.dtype)
-        ring_copy(0, j).start()
-
-    def pass_on(s, carry):
+    for m in range(min(2, hops)):
+        prepare(m)
+    for m in range(hops):
         for j in range(slots):
             at = pl.ds(j * piece, piece)
-            if j == CHUNKS - 2:
-                prepare(s + 1)
-            term = term_of(s, j)
-            ring_copy(s - 1, j).wait_recv()
-            held[s, at, :] = (term + arrived[s - 1, at, :].astype(jnp.float32)).astype(held.dtype)
-            ring_copy(s, j).start()
-        return carry
-
-    lax.fori_loop(1, ring - 1, pass_on, 0)
-    last = ring - 1
+            if j == max(CHUNKS - 2, 0) and m + 2 < ring:
+                prepare(m + 2)
+            term = term_of(m, j)
+            if m >= 2:
+                ring_copy(m - 2, j).wait_recv()
+                term = term + arrived[m - 2, at, :].astype(jnp.float32)
+            held[m, at, :] = term.astype(held.dtype)
+            ring_copy(m, j).start()
+    last = hops
 
     def total_copy(k, j):
         ref = totals.at[line, pl.ds(j * piece, piece), :]
@@ -470,8 +453,10 @@
     for j in range(slots):
         at = pl.ds(j * piece, piece)
         term = term_of(last, j)
-        ring_copy(last - 1, j).wait_recv()
-        value = (term + arrived[last - 1, at, :].astype(jnp.float32)).astype(totals.dtype)
+        for m in range(max(hops - 2, 0), hops):
+            ring_copy(m, j).wait_recv()
+            term = term + arrived[m, at, :].astype(jnp.float32)
+        value = term.astype(totals.dtype)
         if j in shared:
             totals[line, at, :] = value
             for k in range(1, lines):
@@ -494,20 +479,13 @@
         out_across(CHUNKS - 1).wait_recv()
         out_copy(CHUNKS - 1, core).start()
 
-    def finish_cross(s, carry):
-        cross_out(s).wait_send()
+    for m in range(ring):
+        cross_out(m).wait_send()
         if split:
-            lend(s).wait_send()
-        return carry
-
-    lax.fori_loop(0, ring, finish_cross, 0)
-
-    def finish_ring(s, carry):
+            lend(m).wait_send()
+    for m in range(hops):
         for j in range(slots):
-            ring_copy(s, j).wait_send()
-        return carry
-
-    lax.fori_loop(0, ring - 1, finish_ring, 0)
+            ring_copy(m, j).wait_send()
     own.wait()
 
     def finish_gain(k, carry):

time: 123 us -> 113 us (0.919)
  Pallas kernels: 87 us -> 77.5 us
    pallas_call x1, Pallas kernels: 38.6 us -> 32.5 us  [reduce_weight(): pl.pallas_call(functools.partial(reduce_kernel, groups, ring), out_shape=...]
    pallas_call x1, Pallas kernels: 35.3 us -> 31.9 us  [gather_inputs(): pl.pallas_call(functools.partial(gather_kernel, groups, ring), out_shape=...]
where the time goes in v3:
time: 113 us
  Pallas kernels  77.5 us (69%)
  matrix products  12.9 us (11%)
  local copies, waits for them, and re-layouts  10.2 us (9%)
  other arithmetic  9.67 us (9%)
  between operations  2.61 us (2%)
    pallas_call x1, Pallas kernels, reduce_weight(): pl.pallas_call(functools.partial(reduce_kernel, groups, ring), out_shape=...  32.5 us
    pallas_call x1, Pallas kernels, gather_inputs(): pl.pallas_call(functools.partial(gather_kernel, groups, ring), out_shape=...  31.9 us
    pallas_call x1, Pallas kernels, share(): pl.pallas_call(functools.partial(share_kernel, groups, ring), out_shape=j...  13 us
    unnamed x19, local copies, waits for them, and re-layouts  7.36 us
    dot_general x1, matrix products, on_device(): attended = jnp.dot(context, weight_all, preferred_element_type=jnp.float32)  5.35 us
    dot_general x2, matrix products, contract_last(): lax.dot_general(left, right, (((1,), (1,)), ((), ())), preferred_element_...  3.82 us
    reduce_sum x1, other arithmetic, on_device(): gain_part = jnp.sum(normed_grad * stream * inverse_root_mean, axis=0)  3.5 us
    dot_general x2, matrix products, contract_rows(): lax.dot_general(left, right, (((0,), (0,)), ((), ())), preferred_element_...  2.79 us

profile of v3, /device:TPU:0, one launch (start us, length us, event | category | flops | bytes accessed | tf_op | source)
XLA Modules:
  0.0 112.7 jit_solution(14265564077992763259)
XLA Ops:
  0.7 0.7 convert_element_type.38
  1.4 0.7 pad_bitcast_fusion.2
  2.1 0.7 iota_compare_fusion.1
  2.8 0.7 pad_bitcast_fusion
  3.5 1.0 copy-done.1
  4.5 0.8 copy-done.2
  5.3 31.9 %gather_inputs.1 = (bf16[1024,2048]{1,0:T(8,128)(2,1)S(1)}, bf16[32,8,2048]{2,1,0:T(8,128)(2,1)S(1)}, s32[32,8,128]{2,1,0:T(8,128)S(1)}) custom-call(bf16[128,2048]{1,0:T(8,128)(2,1)S(1)} %copy-done.1, bf16[8,2048]{1,0:T(8,128)(2,1)S(1)} %copy-done.2, s32[8,128]{1,0:T(8,128)S(1)} %pad.18.k_in), custom_call_target="tpu_custom_call" | custom-call | tf_op jit(solution)/shard_map/gather_inputs/pallas_call | solution.py:242
  37.2 1.9 %copy-done.3 = bf16[1024,2048]{1,0:T(8,128)(2,1)} copy-done((bf16[1024,2048]{1,0:T(8,128)(2,1)}, bf16[1024,2048]{1,0:T(8,128)(2,1)S(1)}, u32[]{:S(2)}) %copy-start.3) | copy-done | bytes 4194328
  39.2 0.1 log.14
  39.4 0.1 eq.30
  39.6 0.1 select_reduce_fusion.2
  39.7 5.3 %multiply_reduce_fusion = (f32[512]{0:T(512)S(1)}, f32[512,2048]{1,0:T(8,128)S(1)}) fusion(bf16[512,1024]{1,0:T(8,128)(2,1)S(1)} %copy-done, bf16[1024,2048]{1,0:T(8,128)(2,1)} %copy-done.3, bf16[512,2048]{1,0:T(8,128)(2,1)} %param.10), kind=kOutput, calls=%fused_computation.14 | convolution fusion | flops 2151677440 | bytes 11536384 | tf_op jit(solution)/shard_map/dot_general | solution.py:571
  45.1 2.0 %copy-done.5 = f32[512,2048]{1,0:T(8,128)} copy-done((f32[512,2048]{1,0:T(8,128)}, f32[512,2048]{1,0:T(8,128)S(1)}, u32[]{:S(2)}) %copy-start.5) | copy-done | bytes 4194328
  47.1 0.7 select_reduce_fusion
  47.8 0.2 multiply_reduce_fusion.2
  48.0 0.7 multiply_convert_fusion.x_in
  48.7 13.0 %share.1 = bf16[32,2,2048]{2,1,0:T(2,128)(2,1)} custom-call(bf16[2,2048]{1,0:T(2,128)(2,1)} %multiply_convert_fusion.x_in), custom_call_target="tpu_custom_call" | custom-call | tf_op jit(solution)/shard_map/share/pallas_call | solution.py:303
  61.7 1.0 reshape.107
  62.8 0.5 fusion.20
  63.2 0.1 fusion.15
  63.3 0.1 subtract_convert_fusion
  63.4 0.4 multiply_reduce_fusion.1
  63.8 0.9 convolution_convert_fusion
  64.7 0.6 subtract_reduce_fusion
  66.1 3.5 %fusion.8 = (f32[2048]{0:T(1024)S(1)}, f32[512]{0:T(512)S(1)}) fusion(f32[512,2048]{1,0:T(8,128)} %copy-done.5, f32[2,2048]{1,0:T(2,128)S(1)} %subtract_divide_fusion, f32[512]{0:T(512)S(1)} %get-tuple-element.23, pred[512]{0:T(512)(128)(4,1)S(1)} %lt.30, f32[2048]{0:T(1024)S(1)} %copy-done.8), kind=kLoop, calls=%fused_computation.9 | loop fusion | flops 7337472 | bytes 4231680 | tf_op jit(solution)/shard_map/reduce_sum | solution.py:608
  69.6 1.3 %fusion.5 = bf16[512,2048]{1,0:T(8,128)(2,1)S(1)} fusion(f32[512,2048]{1,0:T(8,128)S(1)} %copy-done.6, f32[512]{0:T(512)S(1)} %broadcast_multiply_fusion, f32[512]{0:T(512)S(1)} %get-tuple-element.22, f32[2,2048]{1,0:T(2,128)S(1)} %subtract_divide_fusion, f32[2048]{0:T(1024)S(1)} %copy-done.8, f32[512]{0:T(512)S(1)} %get-tuple-element.23, ...), kind=kLoop, calls=%fused_computation.6 | loop fusion | flops 7340032 | bytes 6322688 | tf_op jit(solution)/shard_map/convert_element_type | solution.py:613
  70.9 0.9 copy-done.4
  71.8 3.4 %convolution_convert_fusion.1 = bf16[512,1024]{1,0:T(8,128)(2,1)} fusion(bf16[512,2048]{1,0:T(8,128)(2,1)S(1)} %fusion.5, bf16[1024,2048]{1,0:T(8,128)(2,1)S(1)} %copy-done.4), kind=kOutput, calls=%fused_computation.16 | convolution fusion | flops 2148007936 | bytes 7340032 | tf_op jit(solution)/shard_map/dot_general | solution.py:23
  75.1 2.4 %convert_bitcast_fusion.part_in = bf16[1024,2048]{1,0:T(8,128)(2,1)S(1)} fusion(bf16[512,2048]{1,0:T(8,128)(2,1)S(1)} %fusion.5, bf16[512,1024]{1,0:T(8,128)(2,1)S(1)} %copy-done), kind=kOutput, calls=%fused_computation.11 | convolution fusion | flops 2149580800 | bytes 7340032 | tf_op jit(solution)/shard_map/dot_general | solution.py:17
  77.5 32.5 %reduce_weight.1 = (bf16[128,2048]{1,0:T(8,128)(2,1)S(1)}, f32[32,1,2048]{2,1,0:T(1,128)S(1)}) custom-call(bf16[1024,2048]{1,0:T(8,128)(2,1)S(1)} %convert_bitcast_fusion.part_in, f32[1,2048]{1,0:T(1,128)S(1)} %bitcast.50), custom_call_target="tpu_custom_call" | custom-call | tf_op jit(solution)/shard_map/reduce_weight/pallas_call | solution.py:513
  110.1 0.8 reduce_sum.109
  110.8 0.8 copy.19
  (25 shorter events, 0.4 us)
Async XLA Ops:
  0.6 39.1 %copy-start = (bf16[512,1024]{1,0:T(8,128)(2,1)S(1)}, bf16[512,1024]{1,0:T(8,128)(2,1)}, u32[]{:S(2)}) copy-start(bf16[512,1024]{1,0:T(8,128)(2,1)} %param.9) | copy-start | bytes 3145732
  3.5 1.0 copy-start.1
  4.5 0.8 copy-start.2
  37.2 1.9 %copy-start.3 = (bf16[1024,2048]{1,0:T(8,128)(2,1)}, bf16[1024,2048]{1,0:T(8,128)(2,1)S(1)}, u32[]{:S(2)}) copy-start(bf16[1024,2048]{1,0:T(8,128)(2,1)S(1)} %get-tuple-element.13) | copy-start | bytes 12582916
  39.7 7.3 %copy-start.8 = (f32[2048]{0:T(1024)S(1)}, f32[2048]{0:T(1024)}, u32[]{:S(2)}) copy-start(f32[2048]{0:T(1024)} %param.12) | copy-start | bytes 24580
  45.1 2.0 %copy-start.5 = (f32[512,2048]{1,0:T(8,128)}, f32[512,2048]{1,0:T(8,128)S(1)}, u32[]{:S(2)}) copy-start(f32[512,2048]{1,0:T(8,128)S(1)} %get-tuple-element.27) | copy-start | bytes 12582916
  66.0 3.6 %copy-start.6 = (f32[512,2048]{1,0:T(8,128)S(1)}, f32[512,2048]{1,0:T(8,128)}, u32[]{:S(2)}) copy-start(f32[512,2048]{1,0:T(8,128)} %copy-done.5) | copy-start | bytes 12582916
  69.6 2.2 %copy-start.4 = (bf16[1024,2048]{1,0:T(8,128)(2,1)S(1)}, bf16[1024,2048]{1,0:T(8,128)(2,1)}, u32[]{:S(2)}) copy-start(bf16[1024,2048]{1,0:T(8,128)(2,1)} %copy-done.3) | copy-start | bytes 12582916
  71.8 3.4 %copy-start.7 = (bf16[512,2048]{1,0:T(8,128)(2,1)}, bf16[512,2048]{1,0:T(8,128)(2,1)S(1)}, u32[]{:S(2)}) copy-start(bf16[512,2048]{1,0:T(8,128)(2,1)S(1)} %fusion.5) | copy-start | bytes 6291460

commit v4 on v3

--- a/solution.py
+++ b/solution.py
@@ -312,8 +312,8 @@
 
 
 def reduce_kernel(
-    groups, ring, part_in, gain_in, out, gain_out,
-    cross, held, arrived, totals, lent, borrowed,
+    groups, ring, context_in, grad_in, weight_in, gain_in, out, gain_out, context_out,
+    part_in, cross, held, arrived, totals, lent, borrowed,
     own_sem, g_send, g_recv, x_send, x_recv, r_send, r_recv, t_send, t_recv, o_send, o_recv,
     y_send, y_recv, f_send, f_recv,
 ):
@@ -348,7 +348,36 @@
             return j
         return CHUNKS - 2 + (line if j == CHUNKS - 2 else 1 - line)
 
-    greet_all(groups, ring, me)
+    barrier = pltpu.get_barrier_semaphore()
+
+    def signal(k, carry):
+        peer = lax.rem(me + k, total)
+        pl.semaphore_signal(
+            barrier, inc=1, device_id=(peer // ring, lax.rem(peer, ring)), device_id_type=MESH
+        )
+        return carry
+
+    lax.fori_loop(1, total, signal, 0)
+    width = part_in.shape[1]
+    wide = width // 2
+
+    def multiply(m):
+        start = pl.multiple_of(owner(m) * rows, rows)
+        left = context_in[:, pl.ds(start, rows)]
+        for t in range(2):
+            at = pl.ds(t * wide, wide)
+            part_in[pl.ds(start, rows), at] = contract_rows(left, grad_in[:, at]).astype(
+                part_in.dtype
+            )
+
+    def context_tile(m):
+        at = pl.ds(m * rows, rows)
+        context_out[:, at] = contract_last(grad_in[...], weight_in[at, :]).astype(
+            context_out.dtype
+        )
+
+    multiply(0)
+    pl.semaphore_wait(barrier, total - 1)
 
     def cross_out(m):
         start = pl.multiple_of(owner(m) * rows + (1 - core) * half, half)
@@ -358,6 +387,8 @@
         )
 
     for m in range(ring):
+        if m > 0:
+            multiply(m)
         cross_out(m).start()
 
     def gain_push(k):
@@ -424,6 +455,7 @@
                 term = term + arrived[m - 2, at, :].astype(jnp.float32)
             held[m, at, :] = term.astype(held.dtype)
             ring_copy(m, j).start()
+        context_tile(m)
     last = hops
 
     def total_copy(k, j):
@@ -466,6 +498,7 @@
             out_across(j).start()
             out_copy(j, core).start()
 
+    context_tile(last)
     for j in shared:
         at = pl.ds(j * piece, piece)
         for k in range(1, lines):
@@ -504,10 +537,11 @@
         out_across(CHUNKS - 2).wait_send()
 
 
-def reduce_weight(groups, ring, partial, gain):
+def reduce_weight(groups, ring, context, grad, weight, gain):
     total = groups * ring
-    rows = partial.shape[0] // ring
-    half, width = rows // 2, partial.shape[1]
+    rows = weight.shape[0] // ring
+    half, width = rows // 2, weight.shape[1]
+    partial = jax.ShapeDtypeStruct(weight.shape, weight.dtype)
     dma = pltpu.SemaphoreType.DMA
     vmem = pl.BlockSpec(memory_space=pltpu.VMEM)
     return pl.pallas_call(
@@ -515,10 +549,12 @@
         out_shape=(
             jax.ShapeDtypeStruct((rows, width), partial.dtype),
             jax.ShapeDtypeStruct((total,) + gain.shape, gain.dtype),
+            jax.ShapeDtypeStruct(context.shape, context.dtype),
         ),
-        in_specs=[vmem, vmem],
-        out_specs=(vmem, vmem),
+        in_specs=[vmem, vmem, vmem, vmem],
+        out_specs=(vmem, vmem, vmem),
         scratch_shapes=[
+            pltpu.VMEM(partial.shape, partial.dtype),
             pltpu.VMEM((ring, half, width), partial.dtype),
             pltpu.VMEM((ring - 1, half, width), partial.dtype),
             pltpu.VMEM((ring - 1, half, width), partial.dtype),
@@ -545,7 +581,7 @@
             collective_id=2, has_side_effects=True, vmem_limit_bytes=40 << 20
         ),
         name="reduce_weight",
-    )(partial, gain)
+    )(context, grad, weight, gain)
 
 
 def on_device(
@@ -611,9 +647,9 @@
         scaled * stream, axis=-1, keepdims=True
     )
     residual_grad = stream_grad.astype(jnp.bfloat16)
-    context_grad = contract_last(residual_grad, weight_all).astype(jnp.bfloat16)
-    partial = contract_rows(context, residual_grad).astype(jnp.bfloat16)
-    weight_grad, gain_all = reduce_weight(groups, ring, partial, gain_part[None, :])
+    weight_grad, gain_all, context_grad = reduce_weight(
+        groups, ring, context, residual_grad, weight_all, gain_part[None, :]
+    )
     gain_grad = jnp.sum(gain_all[:, 0, :], axis=0)
     return (mean_loss, residual_grad, context_grad, weight_grad, gain_grad, user_grad)
 

time: 113 us -> 116 us (1.027)
  matrix products: 12.9 us -> 7.4 us
  Pallas kernels: 77.5 us -> 82.6 us
  local copies, waits for them, and re-layouts: 10.2 us -> 13.3 us
    pallas_call x1, Pallas kernels: 32.5 us -> 37.7 us  [reduce_weight(): pl.pallas_call(functools.partial(reduce_kernel, groups, ring), out_shape=...]
    dot_general x2 -> x1, matrix products: 3.82 us -> 0.46 us  [contract_last(): lax.dot_general(left, right, (((1,), (1,)), ((), ())), preferred_element_...]
    unnamed x19 -> x22, local copies, waits for them, and re-layouts: 7.36 us -> 10.5 us
    dot_general x2 -> x1, matrix products: 2.79 us -> 0.37 us  [contract_rows(): lax.dot_general(left, right, (((0,), (0,)), ((), ())), preferred_element_...]
where the time goes in v4:
time: 116 us
  Pallas kernels  82.6 us (71%)
  local copies, waits for them, and re-layouts  13.3 us (11%)
  other arithmetic  9.57 us (8%)
  matrix products  7.4 us (6%)
  between operations  2.6 us (2%)
    pallas_call x1, Pallas kernels, reduce_weight(): pl.pallas_call(functools.partial(reduce_kernel, groups, ring), out_shape=...  37.7 us
    pallas_call x1, Pallas kernels, gather_inputs(): pl.pallas_call(functools.partial(gather_kernel, groups, ring), out_shape=...  31.9 us
    pallas_call x1, Pallas kernels, share(): pl.pallas_call(functools.partial(share_kernel, groups, ring), out_shape=j...  13 us
    unnamed x22, local copies, waits for them, and re-layouts  10.5 us
    dot_general x1, matrix products, on_device(): attended = jnp.dot(context, weight_all, preferred_element_type=jnp.float32)  5.67 us
    reduce_sum x1, other arithmetic, on_device(): gain_part = jnp.sum(normed_grad * stream * inverse_root_mean, axis=0)  3.49 us

profile of v4, /device:TPU:0, one launch (start us, length us, event | category | flops | bytes accessed | tf_op | source)
XLA Modules:
  0.0 115.5 jit_solution(6423948848004625502)
XLA Ops:
  0.6 0.7 convert_element_type.30
  1.3 0.7 pad_bitcast_fusion.2
  2.0 0.7 iota_compare_fusion.1
  2.7 0.7 pad_bitcast_fusion
  3.4 1.0 copy-done.4
  4.4 0.8 copy-done.6
  5.2 31.9 %gather_inputs.1 = (bf16[1024,2048]{1,0:T(8,128)(2,1)S(1)}, bf16[32,8,2048]{2,1,0:T(8,128)(2,1)S(1)}, s32[32,8,128]{2,1,0:T(8,128)S(1)}) custom-call(bf16[128,2048]{1,0:T(8,128)(2,1)S(1)} %copy-done.4, bf16[8,2048]{1,0:T(8,128)(2,1)S(1)} %copy-done.6, s32[8,128]{1,0:T(8,128)S(1)} %pad.18.k_in), custom_call_target="tpu_custom_call" | custom-call | tf_op jit(solution)/shard_map/gather_inputs/pallas_call | solution.py:242
  37.1 1.9 %copy-done.1 = bf16[1024,2048]{1,0:T(8,128)(2,1)} copy-done((bf16[1024,2048]{1,0:T(8,128)(2,1)}, bf16[1024,2048]{1,0:T(8,128)(2,1)S(1)}, u32[]{:S(2)}) %copy-start.1) | copy-done | bytes 4194328
  39.1 0.1 log.14
  39.3 0.1 eq.30
  39.5 0.1 select_reduce_fusion.2
  39.6 5.7 %multiply_reduce_fusion = (f32[512]{0:T(512)S(1)}, f32[512,2048]{1,0:T(8,128)S(1)}) fusion(bf16[512,1024]{1,0:T(8,128)(2,1)} %context_in.1, bf16[1024,2048]{1,0:T(8,128)(2,1)} %copy-done.1, bf16[512,2048]{1,0:T(8,128)(2,1)} %param.10), kind=kOutput, calls=%fused_computation.13 | convolution fusion | flops 2151677440 | bytes 11536384 | tf_op jit(solution)/shard_map/dot_general | solution.py:607
  45.3 2.0 %copy-done.7 = f32[512,2048]{1,0:T(8,128)} copy-done((f32[512,2048]{1,0:T(8,128)}, f32[512,2048]{1,0:T(8,128)S(1)}, u32[]{:S(2)}) %copy-start.7) | copy-done | bytes 4194328
  47.3 0.7 select_reduce_fusion
  48.0 0.2 multiply_reduce_fusion.2
  48.2 0.7 multiply_convert_fusion.x_in
  48.9 13.0 %share.1 = bf16[32,2,2048]{2,1,0:T(2,128)(2,1)} custom-call(bf16[2,2048]{1,0:T(2,128)(2,1)} %multiply_convert_fusion.x_in), custom_call_target="tpu_custom_call" | custom-call | tf_op jit(solution)/shard_map/share/pallas_call | solution.py:303
  61.9 1.0 reshape.107
  63.0 0.5 fusion.20
  63.4 0.1 fusion.15
  63.6 0.4 multiply_reduce_fusion.1
  64.0 0.9 convolution_convert_fusion
  64.9 0.6 subtract_reduce_fusion
  66.3 3.5 %fusion.8 = (f32[2048]{0:T(1024)S(1)}, f32[512]{0:T(512)S(1)}) fusion(f32[512,2048]{1,0:T(8,128)} %copy-done.7, f32[2,2048]{1,0:T(2,128)S(1)} %subtract_divide_fusion, f32[512]{0:T(512)S(1)} %get-tuple-element.25, pred[512]{0:T(512)(128)(4,1)S(1)} %lt.30, f32[2048]{0:T(1024)S(1)} %copy-done.9), kind=kLoop, calls=%fused_computation.9 | loop fusion | flops 7337472 | bytes 4231680 | tf_op jit(solution)/shard_map/reduce_sum | solution.py:644
  69.8 1.3 %fusion.5.grad_in = bf16[512,2048]{1,0:T(8,128)(2,1)S(1)} fusion(f32[512,2048]{1,0:T(8,128)S(1)} %copy-done.8, f32[512]{0:T(512)S(1)} %broadcast_multiply_fusion, f32[512]{0:T(512)S(1)} %get-tuple-element.24, f32[2,2048]{1,0:T(2,128)S(1)} %subtract_divide_fusion, f32[2048]{0:T(1024)S(1)} %copy-done.9, f32[512]{0:T(512)S(1)} %get-tuple-element.25, ...), kind=kLoop, calls=%fused_computation.6 | loop fusion | flops 7340032 | bytes 6322688 | tf_op jit(solution)/shard_map/convert_element_type | solution.py:649
  71.1 0.9 copy-done.2
  72.0 0.3 copy-done.3
  72.3 37.7 %reduce_weight.1 = (bf16[128,2048]{1,0:T(8,128)(2,1)S(1)}, f32[32,1,2048]{2,1,0:T(1,128)S(1)}, bf16[512,1024]{1,0:T(8,128)(2,1)S(1)}) custom-call(bf16[512,1024]{1,0:T(8,128)(2,1)S(1)} %copy-done.3, bf16[512,2048]{1,0:T(8,128)(2,1)S(1)} %fusion.5.grad_in, bf16[1024,2048]{1,0:T(8,128)(2,1)S(1)} %copy-done.2, f32[1,2048]{1,0:T(1,128)S(1)} %bitcast.44), custom_call_target="tpu_custom_call" | custom-call | tf_op jit(solution)/shard_map/reduce_weight/pallas_call | solution.py:547
  110.0 0.8 copy-done.5
  110.8 0.8 reduce_sum.109
  111.5 1.0 copy.17
  112.5 1.9 %copy.18 = bf16[128,2048]{1,0:T(8,128)(2,1)} copy(bf16[128,2048]{1,0:T(8,128)(2,1)} %copy-done.5) | data formatting | bytes 1048576
  (26 shorter events, 0.5 us)
Async XLA Ops:
  3.4 1.0 copy-start.4
  4.4 0.8 copy-start.6
  37.1 1.9 %copy-start.1 = (bf16[1024,2048]{1,0:T(8,128)(2,1)}, bf16[1024,2048]{1,0:T(8,128)(2,1)S(1)}, u32[]{:S(2)}) copy-start(bf16[1024,2048]{1,0:T(8,128)(2,1)S(1)} %get-tuple-element.14.weight_in) | copy-start | bytes 12582916
  39.6 7.7 %copy-start.9 = (f32[2048]{0:T(1024)S(1)}, f32[2048]{0:T(1024)}, u32[]{:S(2)}) copy-start(f32[2048]{0:T(1024)} %param.12) | copy-start | bytes 24580
  45.3 2.0 %copy-start.7 = (f32[512,2048]{1,0:T(8,128)}, f32[512,2048]{1,0:T(8,128)S(1)}, u32[]{:S(2)}) copy-start(f32[512,2048]{1,0:T(8,128)S(1)} %get-tuple-element.29) | copy-start | bytes 12582916
  66.2 3.6 %copy-start.8 = (f32[512,2048]{1,0:T(8,128)S(1)}, f32[512,2048]{1,0:T(8,128)}, u32[]{:S(2)}) copy-start(f32[512,2048]{1,0:T(8,128)} %copy-done.7) | copy-start | bytes 12582916
  69.8 2.2 %copy-start.2 = (bf16[1024,2048]{1,0:T(8,128)(2,1)S(1)}, bf16[1024,2048]{1,0:T(8,128)(2,1)}, u32[]{:S(2)}) copy-start(bf16[1024,2048]{1,0:T(8,128)(2,1)} %copy-done.1) | copy-start | bytes 12582916
  69.8 2.5 %copy-start.3 = (bf16[512,1024]{1,0:T(8,128)(2,1)S(1)}, bf16[512,1024]{1,0:T(8,128)(2,1)}, u32[]{:S(2)}) copy-start(bf16[512,1024]{1,0:T(8,128)(2,1)} %context_in.1) | copy-start | bytes 3145732
  72.3 40.2 %copy-start = (bf16[512,2048]{1,0:T(8,128)(2,1)}, bf16[512,2048]{1,0:T(8,128)(2,1)S(1)}, u32[]{:S(2)}) copy-start(bf16[512,2048]{1,0:T(8,128)(2,1)S(1)} %fusion.5.grad_in) | copy-start | bytes 6291460
  110.0 0.8 copy-start.5

commit v5 on v3

--- a/solution.py
+++ b/solution.py
@@ -261,39 +261,39 @@
     )(weight, users, keys)
 
 
-def share_kernel(groups, ring, x_in, x_out, own_sem, send_sem, recv_sem):
-    total = groups * ring
-    me = lax.axis_index("dp") * ring + lax.axis_index("fsdp")
-    greet_all(groups, ring, me)
-
-    def push(k):
-        peer = lax.rem(me + k, total)
+def share_kernel(groups, ring, x_in, x_out, own_sem, send_sem, recv_sem, wide_send, wide_recv):
+    group, index = lax.axis_index("dp"), lax.axis_index("fsdp")
+    greet(
+        [(group, lax.rem(index + k, ring)) for k in range(1, ring)]
+        + [(lax.rem(group + k, groups), index) for k in range(1, groups)]
+    )
+
+    def along(k, source):
         return remote(
-            x_in, x_out.at[me], send_sem.at[k - 1], recv_sem.at[k - 1],
-            (peer // ring, lax.rem(peer, ring)),
-        )
-
-    def pull(k):
-        source = lax.rem(me + total - k, total)
+            x_in, x_out.at[group * ring + source], send_sem.at[k - 1], recv_sem.at[k - 1],
+            (group, lax.rem(index + k, ring)),
+        )
+
+    def wide(k, source):
+        ref = x_out.at[pl.ds(source * ring, ring)]
         return remote(
-            x_in, x_out.at[source], send_sem.at[k - 1], recv_sem.at[k - 1],
-            (source // ring, lax.rem(source, ring)),
-        )
-
-    def start(k, carry):
-        push(k).start()
-        return carry
-
-    def finish(k, carry):
-        push(k).wait_send()
-        pull(k).wait_recv()
-        return carry
-
-    lax.fori_loop(1, total, start, 0)
-    own = pltpu.make_async_copy(x_in, x_out.at[me], own_sem)
+            ref, ref, wide_send.at[k - 1], wide_recv.at[k - 1], (lax.rem(group + k, groups), index)
+        )
+
+    for k in range(1, ring):
+        along(k, index).start()
+    own = pltpu.make_async_copy(x_in, x_out.at[group * ring + index], own_sem)
     own.start()
     own.wait()
-    lax.fori_loop(1, total, finish, 0)
+    for k in range(1, ring):
+        along(k, lax.rem(index + ring - k, ring)).wait_recv()
+    for k in range(1, groups):
+        wide(k, group).start()
+    for k in range(1, ring):
+        along(k, index).wait_send()
+    for k in range(1, groups):
+        wide(k, group).wait_send()
+        wide(k, lax.rem(group + groups - k, groups)).wait_recv()
 
 
 def share(groups, ring, block):
@@ -305,7 +305,7 @@
         out_shape=jax.ShapeDtypeStruct((total,) + block.shape, block.dtype),
         in_specs=[vmem],
         out_specs=vmem,
-        scratch_shapes=[dma, dma((total - 1,)), dma((total - 1,))],
+        scratch_shapes=[dma] + [dma((ring - 1,))] * 2 + [dma((groups - 1,))] * 2,
         compiler_params=pltpu.CompilerParams(collective_id=1, has_side_effects=True),
         name="share",
     )(block)
@@ -558,16 +558,14 @@
     item_length = tok_rows // items_here
     users_here = user_vectors.shape[0]
     devices_all = groups * ring
-    lanes = 128 * pl.cdiv(max(users_here, items_here), 128)
-    keys = jnp.stack(
-        [jnp.pad(row, (0, lanes - row.shape[0])) for row in (positive, item_ids, item_counts)]
-    )
-    keys = jnp.pad(keys, ((0, 5), (0, 0)))
+    keys = jnp.concatenate([positive, item_ids, item_counts])
+    lanes = 128 * pl.cdiv(keys.shape[0], 128)
+    keys = jnp.broadcast_to(jnp.pad(keys, (0, lanes - keys.shape[0]))[None, :], (8, lanes))
     weight_all, users_all, keys_all = gather_inputs(groups, ring, out_weight, user_vectors, keys)
     users_all = users_all.reshape(devices_all * users_here, model_width)
     positive_all = keys_all[:, 0, :users_here].reshape(-1)
-    ids_all = keys_all[:, 1, :items_here].reshape(-1)
-    counts_all = keys_all[:, 2, :items_here].reshape(-1)
+    ids_all = keys_all[:, 0, users_here : users_here + items_here].reshape(-1)
+    counts_all = keys_all[:, 0, users_here + items_here : users_here + 2 * items_here].reshape(-1)
     attended = jnp.dot(context, weight_all, preferred_element_type=jnp.float32)
     stream = residual.astype(jnp.float32) + attended
     inverse_root_mean = lax.rsqrt(jnp.mean(stream * stream, axis=-1, keepdims=True) + EPSILON)

time: 113 us -> 112 us (level)
  local copies, waits for them, and re-layouts: 10.2 us -> 8.89 us
    pallas_call x1, Pallas kernels: 13 us -> 11.5 us  [share(): pl.pallas_call(functools.partial(share_kernel, groups, ring), out_shape=j...]
    another operation x2 -> x0, local copies, waits for them, and re-layouts: 1.33 us -> none  [on_device(): jnp.stack([jnp.pad(row, (0, lanes - row.shape[0])) for row in (positive,...]
where the time goes in v5:
time: 112 us; the launch traced here: 111 us
  Pallas kernels  76.4 us (68%)
  matrix products  12.9 us (12%)
  other arithmetic  10.5 us (9%)
  local copies, waits for them, and re-layouts  8.89 us (8%)
  between operations  2.61 us (2%)
    pallas_call x1, Pallas kernels, reduce_weight(): pl.pallas_call(functools.partial(reduce_kernel, groups, ring), out_shape=...  32.9 us
    pallas_call x1, Pallas kernels, gather_inputs(): pl.pallas_call(functools.partial(gather_kernel, groups, ring), out_shape=...  31.9 us
    pallas_call x1, Pallas kernels, share(): pl.pallas_call(functools.partial(share_kernel, groups, ring), out_shape=j...  11.5 us
    unnamed x19, local copies, waits for them, and re-layouts  7.36 us
    dot_general x1, matrix products, on_device(): attended = jnp.dot(context, weight_all, preferred_element_type=jnp.float32)  5.35 us
    dot_general x2, matrix products, contract_last(): lax.dot_general(left, right, (((1,), (1,)), ((), ())), preferred_element_...  3.82 us
    reduce_sum x1, other arithmetic, on_device(): gain_part = jnp.sum(normed_grad * stream * inverse_root_mean, axis=0)  3.5 us
    dot_general x2, matrix products, contract_rows(): lax.dot_general(left, right, (((0,), (0,)), ((), ())), preferred_element_...  2.79 us

profile of v5, /device:TPU:0, one launch (start us, length us, event | category | flops | bytes accessed | tf_op | source)
XLA Modules:
  0.0 111.2 jit_solution(10701640069859742246)
XLA Ops:
  0.7 0.7 convert_element_type.38
  1.4 0.8 pad_add_fusion
  2.2 0.7 iota_compare_fusion.1
  2.9 1.0 copy-done.1
  4.0 0.8 copy-done.2
  4.7 31.9 %gather_inputs.1 = (bf16[1024,2048]{1,0:T(8,128)(2,1)S(1)}, bf16[32,8,2048]{2,1,0:T(8,128)(2,1)S(1)}, s32[32,8,128]{2,1,0:T(8,128)S(1)}) custom-call(bf16[128,2048]{1,0:T(8,128)(2,1)S(1)} %copy-done.1, bf16[8,2048]{1,0:T(8,128)(2,1)S(1)} %copy-done.2, s32[8,128]{1,0:T(8,128)S(1)} %broadcast_in_dim.78.k_in), custom_call_target="tpu_custom_call" | custom-call | tf_op jit(solution)/shard_map/gather_inputs/pallas_call | solution.py:242
  36.7 1.9 %copy-done.3 = bf16[1024,2048]{1,0:T(8,128)(2,1)} copy-done((bf16[1024,2048]{1,0:T(8,128)(2,1)}, bf16[1024,2048]{1,0:T(8,128)(2,1)S(1)}, u32[]{:S(2)}) %copy-start.3) | copy-done | bytes 4194328
  38.6 0.1 log_reduce_fusion
  38.7 0.1 log.14
  38.9 0.1 slice_reduce_fusion.1
  39.0 0.1 eq.30
  39.2 0.1 select_reduce_fusion.2
  39.3 5.3 %multiply_reduce_fusion = (f32[512]{0:T(512)S(1)}, f32[512,2048]{1,0:T(8,128)S(1)}) fusion(bf16[512,1024]{1,0:T(8,128)(2,1)S(1)} %copy-done, bf16[1024,2048]{1,0:T(8,128)(2,1)} %copy-done.3, bf16[512,2048]{1,0:T(8,128)(2,1)} %param.10), kind=kOutput, calls=%fused_computation.14 | convolution fusion | flops 2151677440 | bytes 11536384 | tf_op jit(solution)/shard_map/dot_general | solution.py:569
  44.7 2.0 %copy-done.5 = f32[512,2048]{1,0:T(8,128)} copy-done((f32[512,2048]{1,0:T(8,128)}, f32[512,2048]{1,0:T(8,128)S(1)}, u32[]{:S(2)}) %copy-start.5) | copy-done | bytes 4194328
  46.6 0.7 select_reduce_fusion
  47.3 0.2 multiply_reduce_fusion.2
  47.5 0.7 multiply_convert_fusion.x_in
  48.2 11.5 %share.1 = bf16[32,2,2048]{2,1,0:T(2,128)(2,1)} custom-call(bf16[2,2048]{1,0:T(2,128)(2,1)} %multiply_convert_fusion.x_in), custom_call_target="tpu_custom_call" | custom-call | tf_op jit(solution)/shard_map/share/pallas_call | solution.py:303
  59.8 1.0 reshape.108
  60.8 0.5 fusion.20
  61.3 0.1 fusion.15
  61.5 0.4 multiply_reduce_fusion.1
  61.9 0.9 convolution_convert_fusion
  62.7 0.6 subtract_reduce_fusion
  64.1 3.5 %fusion.8 = (f32[2048]{0:T(1024)S(1)}, f32[512]{0:T(512)S(1)}) fusion(f32[512,2048]{1,0:T(8,128)} %copy-done.5, f32[2,2048]{1,0:T(2,128)S(1)} %subtract_divide_fusion, f32[512]{0:T(512)S(1)} %get-tuple-element.23, pred[512]{0:T(512)(128)(4,1)S(1)} %lt.30, f32[2048]{0:T(1024)S(1)} %copy-done.8), kind=kLoop, calls=%fused_computation.9 | loop fusion | flops 7337472 | bytes 4231680 | tf_op jit(solution)/shard_map/reduce_sum | solution.py:606
  67.6 1.3 %fusion.5 = bf16[512,2048]{1,0:T(8,128)(2,1)S(1)} fusion(f32[512,2048]{1,0:T(8,128)S(1)} %copy-done.6, f32[512]{0:T(512)S(1)} %broadcast_multiply_fusion, f32[512]{0:T(512)S(1)} %get-tuple-element.22, f32[2,2048]{1,0:T(2,128)S(1)} %subtract_divide_fusion, f32[2048]{0:T(1024)S(1)} %copy-done.8, f32[512]{0:T(512)S(1)} %get-tuple-element.23, ...), kind=kLoop, calls=%fused_computation.6 | loop fusion | flops 7340032 | bytes 6322688 | tf_op jit(solution)/shard_map/convert_element_type | solution.py:611
  68.9 0.9 copy-done.4
  69.8 3.4 %convolution_convert_fusion.1 = bf16[512,1024]{1,0:T(8,128)(2,1)} fusion(bf16[512,2048]{1,0:T(8,128)(2,1)S(1)} %fusion.5, bf16[1024,2048]{1,0:T(8,128)(2,1)S(1)} %copy-done.4), kind=kOutput, calls=%fused_computation.16 | convolution fusion | flops 2148007936 | bytes 7340032 | tf_op jit(solution)/shard_map/dot_general | solution.py:23
  73.2 2.4 %convert_bitcast_fusion.part_in = bf16[1024,2048]{1,0:T(8,128)(2,1)S(1)} fusion(bf16[512,2048]{1,0:T(8,128)(2,1)S(1)} %fusion.5, bf16[512,1024]{1,0:T(8,128)(2,1)S(1)} %copy-done), kind=kOutput, calls=%fused_computation.11 | convolution fusion | flops 2149580800 | bytes 7340032 | tf_op jit(solution)/shard_map/dot_general | solution.py:17
  75.6 32.9 %reduce_weight.1 = (bf16[128,2048]{1,0:T(8,128)(2,1)S(1)}, f32[32,1,2048]{2,1,0:T(1,128)S(1)}) custom-call(bf16[1024,2048]{1,0:T(8,128)(2,1)S(1)} %convert_bitcast_fusion.part_in, f32[1,2048]{1,0:T(1,128)S(1)} %bitcast.44), custom_call_target="tpu_custom_call" | custom-call | tf_op jit(solution)/shard_map/reduce_weight/pallas_call | solution.py:513
  108.5 0.8 reduce_sum.109
  109.3 0.8 copy.19
  (24 shorter events, 0.4 us)
Async XLA Ops:
  0.6 38.6 %copy-start = (bf16[512,1024]{1,0:T(8,128)(2,1)S(1)}, bf16[512,1024]{1,0:T(8,128)(2,1)}, u32[]{:S(2)}) copy-start(bf16[512,1024]{1,0:T(8,128)(2,1)} %param.9) | copy-start | bytes 3145732
  2.9 1.0 copy-start.1
  4.0 0.8 copy-start.2
  36.6 1.9 %copy-start.3 = (bf16[1024,2048]{1,0:T(8,128)(2,1)}, bf16[1024,2048]{1,0:T(8,128)(2,1)S(1)}, u32[]{:S(2)}) copy-start(bf16[1024,2048]{1,0:T(8,128)(2,1)S(1)} %get-tuple-element.13) | copy-start | bytes 12582916
  39.3 7.3 %copy-start.8 = (f32[2048]{0:T(1024)S(1)}, f32[2048]{0:T(1024)}, u32[]{:S(2)}) copy-start(f32[2048]{0:T(1024)} %param.12) | copy-start | bytes 24580
  44.6 2.0 %copy-start.5 = (f32[512,2048]{1,0:T(8,128)}, f32[512,2048]{1,0:T(8,128)S(1)}, u32[]{:S(2)}) copy-start(f32[512,2048]{1,0:T(8,128)S(1)} %get-tuple-element.27) | copy-start | bytes 12582916
  64.0 3.6 %copy-start.6 = (f32[512,2048]{1,0:T(8,128)S(1)}, f32[512,2048]{1,0:T(8,128)}, u32[]{:S(2)}) copy-start(f32[512,2048]{1,0:T(8,128)} %copy-done.5) | copy-start | bytes 12582916
  67.6 2.2 %copy-start.4 = (bf16[1024,2048]{1,0:T(8,128)(2,1)S(1)}, bf16[1024,2048]{1,0:T(8,128)(2,1)}, u32[]{:S(2)}) copy-start(bf16[1024,2048]{1,0:T(8,128)(2,1)} %copy-done.3) | copy-start | bytes 12582916
  69.8 3.4 %copy-start.7 = (bf16[512,2048]{1,0:T(8,128)(2,1)}, bf16[512,2048]{1,0:T(8,128)(2,1)S(1)}, u32[]{:S(2)}) copy-start(bf16[512,2048]{1,0:T(8,128)(2,1)S(1)} %fusion.5) | copy-start | bytes 6291460
